TPU v7x, 32 devices: a whole 2x2x4 slice. The times are simulated.
32 devices in a mesh: fsdp: 2 (over y), ctx: 4 (over z), tp: 4 (over x, core).
Axes of the slice: x: 2, y: 2, z: 4, core: 2. Of those that a mesh axis runs over, the one named last changes fastest.
Arguments:
- hidden_in: bfloat16 [2, 1024, 576], P('fsdp', 'ctx'), may hold values from -6 to 6
- segments: int32 [2, 1024], P('fsdp', 'ctx'), may hold values from 0 to 4, as said below
- positions: int32 [2, 1024], P('fsdp', 'ctx'), may hold values from 0 to 511, as said below
- attn_gain: bfloat16 [576], P('fsdp')
- query_weight: bfloat16 [576, 576], P('fsdp'), may hold values from -0.25 to 0.25
- kv_weight: bfloat16 [576, 384], P('fsdp'), may hold values from -0.25 to 0.25
- out_weight: bfloat16 [576, 576], P('fsdp'), may hold values from -1 to 1
- mlp_gain: bfloat16 [576], P('fsdp'), may hold values from 0.25 to 1.75
- gate_up_weight: bfloat16 [576, 2, 1536], P('fsdp', None, 'tp'), may hold values from -0.25 to 0.25
- down_weight: bfloat16 [576, 1536], P('fsdp', 'tp'), may hold values from -0.15625 to 0.15625
- cotangent: bfloat16 [2, 1024, 576], P('fsdp', 'ctx'), may hold values from -6 to 6
Outputs:
- block_output: bfloat16 [2, 1024, 576], P('fsdp', 'ctx')
- input_grad: float32 [2, 1024, 576], P('fsdp', 'ctx')
- attn_gain_grad: float32 [576], P('fsdp')
- query_weight_grad: float32 [576, 576], P('fsdp')
- kv_weight_grad: float32 [576, 384], P('fsdp')
- out_weight_grad: float32 [576, 576], P('fsdp')
- mlp_gain_grad: float32 [576], P('fsdp')
- gate_up_weight_grad: float32 [576, 2, 1536], P('fsdp', None, 'tp')
- down_weight_grad: float32 [576, 1536], P('fsdp', 'tp')
Inputs may be any that keep to these rules, and one draw needn't show every extreme that they name: `segments`: each sequence holds 2 to 5 documents, numbered from 0 in order and filling the whole sequence; the segment number never falls and rises by at most one from one token to the next; each document has 102 tokens or more. `positions`: each token's position is the number of tokens before it in its own segment of its sequence; every sequence has a document of exactly 512 tokens, and none is longer.
All inputs are finite; a program needn't handle non-finite values.
Results may differ from a plain program's by a relative error of at most 0.02.
The roundings to bfloat16 on the way count: a program that leaves them out, or rounds other values in their place, can miss the bound.
Values may be sent and summed in bfloat16 or wider, within the bound.
A program may use at most 64 MiB of HBM per device.

v0:
```python
import jax
import jax.numpy as jnp
from jax import lax
from jax.sharding import PartitionSpec as P

D = 576
H = 9
KV = 3
HD = 64


eps = 1e-05
theta = 100000.0
neg_fill = -1e30


def rotary_tables(doc_positions):
    freq_index = jnp.arange(HD // 2, dtype=jnp.float32)
    inverse_freq = theta ** (-2.0 * freq_index / HD)
    angles = doc_positions.astype(jnp.float32)[:, None] * inverse_freq[None, :]
    return (jnp.cos(angles)[:, None, :], jnp.sin(angles)[:, None, :])


def rotate(tensor, cos_table, sin_table):
    lower_half = tensor[..., : HD // 2]
    upper_half = tensor[..., HD // 2 :]
    return jnp.concatenate(
        [
            lower_half * cos_table - upper_half * sin_table,
            upper_half * cos_table + lower_half * sin_table,
        ],
        axis=-1,
    )


def unrotate(tensor, cos_table, sin_table):
    lower_half = tensor[..., : HD // 2]
    upper_half = tensor[..., HD // 2 :]
    return jnp.concatenate(
        [
            lower_half * cos_table + upper_half * sin_table,
            upper_half * cos_table - lower_half * sin_table,
        ],
        axis=-1,
    )


def norm_forward(stream, gain_row):
    inv_rms = lax.rsqrt(jnp.mean(stream * stream, axis=-1, keepdims=True) + eps)
    return (inv_rms, (stream * inv_rms * gain_row.astype(jnp.float32)).astype(jnp.bfloat16))


def norm_backward(stream, inv_rms, gain_row, grad_normed):
    scaled = grad_normed * gain_row.astype(jnp.float32)
    gain_grad = jnp.sum(grad_normed * stream * inv_rms, axis=0)
    stream_grad = inv_rms * scaled - stream * inv_rms**3 * jnp.mean(
        scaled * stream, axis=-1, keepdims=True
    )
    return (gain_grad, stream_grad)


def key_layout(keys_all, values_all, key_segs):
    length = keys_all.shape[0]
    block_len = 512
    block_count = length // block_len
    starts = jnp.arange(block_count, dtype=jnp.int32) * block_len
    return (
        keys_all.reshape(block_count, block_len, KV, HD),
        values_all.reshape(block_count, block_len, KV, HD),
        key_segs.reshape(block_count, block_len),
        starts,
    )


def visible_mask(block_start, seg_block, query_index, query_segs):
    key_index = block_start + jnp.arange(seg_block.shape[0], dtype=jnp.int32)
    return (query_segs[:, None] == seg_block[None, :]) & (
        key_index[None, :] <= query_index[:, None]
    )


def group_scores(query_group, key_group):
    return jnp.einsum(
        "tgd,kd->gtk", query_group, key_group, preferred_element_type=jnp.float32
    ) * HD ** (-0.5)


def attention_forward(queries, layout, query_index, query_segs):
    key_blocks, value_blocks, seg_blocks, starts = layout
    row_count = queries.shape[0]
    groups = H // KV

    def stats_block(running, inputs):
        key_block, seg_block, block_start = inputs
        visible = visible_mask(block_start, seg_block, query_index, query_segs)[None]
        row_tops, totals = running
        new_tops = []
        new_totals = []
        for kv_group in range(KV):
            scores = jnp.where(
                visible, group_scores(queries[:, kv_group], key_block[:, kv_group]), neg_fill
            )
            group_top = jnp.maximum(row_tops[kv_group], jnp.max(scores, axis=-1))
            weight_sum = jnp.sum(
                jnp.where(visible, jnp.exp(scores - group_top[..., None]), 0.0), axis=-1
            )
            new_tops.append(group_top)
            new_totals.append(
                totals[kv_group] * jnp.exp(row_tops[kv_group] - group_top) + weight_sum
            )
        return ((jnp.stack(new_tops), jnp.stack(new_totals)), None)

    start_top = jnp.full((KV, groups, row_count), neg_fill, jnp.float32)
    start_total = jnp.zeros((KV, groups, row_count), jnp.float32)
    (row_tops, totals), unused = lax.scan(
        stats_block, (start_top, start_total), (key_blocks, seg_blocks, starts)
    )
    log_norm = row_tops + jnp.log(totals)

    def output_block(accumulated, inputs):
        key_block, value_block, seg_block, block_start = inputs
        visible = visible_mask(block_start, seg_block, query_index, query_segs)[None]
        value_parts = []
        for kv_group in range(KV):
            scores = jnp.where(
                visible, group_scores(queries[:, kv_group], key_block[:, kv_group]), neg_fill
            )
            attn_probs = jnp.where(
                visible, jnp.exp(scores - log_norm[kv_group][..., None]), 0.0
            ).astype(jnp.bfloat16)
            value_parts.append(
                jnp.einsum(
                    "gtk,kd->tgd",
                    attn_probs,
                    value_block[:, kv_group],
                    preferred_element_type=jnp.float32,
                )
            )
        return (accumulated + jnp.stack(value_parts, axis=1), None)

    accumulated, unused = lax.scan(
        output_block,
        jnp.zeros((row_count, KV, groups, HD), jnp.float32),
        (key_blocks, value_blocks, seg_blocks, starts),
    )
    return (accumulated.astype(jnp.bfloat16), log_norm)


def attention_backward(queries, layout, query_index, query_segs, log_norm, grad_out, row_delta):
    key_blocks, value_blocks, seg_blocks, starts = layout
    row_count = queries.shape[0]
    groups = H // KV
    score_scale = HD ** (-0.5)

    def grad_block(grad_query, inputs):
        key_block, value_block, seg_block, block_start = inputs
        visible = visible_mask(block_start, seg_block, query_index, query_segs)[None]
        query_parts = []
        key_parts = []
        value_parts = []
        for kv_group in range(KV):
            scores = jnp.where(
                visible, group_scores(queries[:, kv_group], key_block[:, kv_group]), neg_fill
            )
            attn_probs = jnp.where(visible, jnp.exp(scores - log_norm[kv_group][..., None]), 0.0)
            grad_probs = jnp.einsum(
                "tgd,kd->gtk",
                grad_out[:, kv_group],
                value_block[:, kv_group],
                preferred_element_type=jnp.float32,
            )
            grad_scores = (attn_probs * (grad_probs - row_delta[kv_group][..., None])).astype(
                jnp.bfloat16
            )
            value_parts.append(
                jnp.einsum(
                    "gtk,tgd->kd",
                    attn_probs.astype(jnp.bfloat16),
                    grad_out[:, kv_group],
                    preferred_element_type=jnp.float32,
                )
            )
            key_parts.append(
                jnp.einsum(
                    "gtk,tgd->kd",
                    grad_scores,
                    queries[:, kv_group],
                    preferred_element_type=jnp.float32,
                )
                * score_scale
            )
            query_parts.append(
                jnp.einsum(
                    "gtk,kd->tgd",
                    grad_scores,
                    key_block[:, kv_group],
                    preferred_element_type=jnp.float32,
                )
                * score_scale
            )
        return (
            grad_query + jnp.stack(query_parts, axis=1),
            (jnp.stack(key_parts, axis=1), jnp.stack(value_parts, axis=1)),
        )

    grad_query, (grad_keys, grad_values) = lax.scan(
        grad_block,
        jnp.zeros((row_count, KV, groups, HD), jnp.float32),
        (key_blocks, value_blocks, seg_blocks, starts),
    )
    return (grad_query, grad_keys.reshape(-1, KV, HD), grad_values.reshape(-1, KV, HD))


def shards(
    hidden_in,
    segments,
    positions,
    attn_gain,
    query_weight,
    kv_weight,
    out_weight,
    mlp_gain,
    gate_up_weight,
    down_weight,
    cotangent,
):
    groups = H // KV
    row_count = hidden_in.shape[1]
    stream = hidden_in.reshape(row_count, D).astype(jnp.float32)
    query_segs = segments.reshape(row_count)
    doc_pos = positions.reshape(row_count)
    full_attn_gain, full_query, full_kv, full_out, full_mlp_gain, full_gate_up, full_down = (
        lax.all_gather(attn_gain, "fsdp", axis=0, tiled=True),
        lax.all_gather(query_weight, "fsdp", axis=0, tiled=True),
        lax.all_gather(kv_weight, "fsdp", axis=0, tiled=True),
        lax.all_gather(out_weight, "fsdp", axis=0, tiled=True),
        lax.all_gather(mlp_gain, "fsdp", axis=0, tiled=True),
        lax.all_gather(gate_up_weight, "fsdp", axis=0, tiled=True),
        lax.all_gather(down_weight, "fsdp", axis=0, tiled=True),
    )
    cos_table, sin_table = rotary_tables(doc_pos)
    inv_first, normed_first = norm_forward(stream, full_attn_gain)
    query_raw = jnp.dot(normed_first, full_query, preferred_element_type=jnp.float32).reshape(
        row_count, H, HD
    )
    queries = (
        rotate(query_raw, cos_table, sin_table)
        .astype(jnp.bfloat16)
        .reshape(row_count, KV, groups, HD)
    )
    kv_raw = jnp.dot(normed_first, full_kv, preferred_element_type=jnp.float32).reshape(
        row_count, 2, KV, HD
    )
    kv_local = (
        jnp.stack([rotate(kv_raw[:, 0], cos_table, sin_table), kv_raw[:, 1]], axis=1)
        .astype(jnp.bfloat16)
        .reshape(row_count, 2 * KV * HD)
    )
    kv_all = lax.all_gather(kv_local, "ctx", axis=0, tiled=True)
    key_segs = lax.all_gather(query_segs, "ctx", axis=0, tiled=True)
    kv_view = kv_all.reshape(-1, 2, KV, HD)
    layout = key_layout(kv_view[:, 0], kv_view[:, 1], key_segs)
    query_index = lax.axis_index("ctx") * row_count + jnp.arange(row_count, dtype=jnp.int32)
    attended, log_norm = attention_forward(queries, layout, query_index, query_segs)
    attended_flat = attended.reshape(row_count, H * HD)
    mid_stream = stream + jnp.dot(attended_flat, full_out, preferred_element_type=jnp.float32)
    inv_second, normed_second = norm_forward(mid_stream, full_mlp_gain)
    gate_up = jnp.einsum(
        "td,dcf->tcf", normed_second, full_gate_up, preferred_element_type=jnp.float32
    )
    gate_value = gate_up[:, 0]
    up_part = gate_up[:, 1]
    gate_sigmoid = jax.nn.sigmoid(gate_value)
    hidden_act = (gate_value * gate_sigmoid * up_part).astype(jnp.bfloat16)
    partial_down = jnp.einsum(
        "tf,df->td", hidden_act, full_down, preferred_element_type=jnp.float32
    )
    mlp_out = lax.psum(partial_down.astype(jnp.bfloat16), "tp").astype(jnp.float32)
    block_out = (mid_stream + mlp_out).astype(jnp.bfloat16).reshape(1, row_count, D)
    grad_top = cotangent.reshape(row_count, D)
    down_grad = jnp.einsum("td,tf->df", grad_top, hidden_act, preferred_element_type=jnp.float32)
    grad_hidden = jnp.einsum("td,df->tf", grad_top, full_down, preferred_element_type=jnp.float32)
    grad_gate = grad_hidden * up_part * gate_sigmoid * (1.0 + gate_value * (1.0 - gate_sigmoid))
    grad_up = grad_hidden * gate_value * gate_sigmoid
    grad_gu = jnp.stack([grad_gate, grad_up], axis=1).astype(jnp.bfloat16)
    gate_up_grad = jnp.einsum(
        "td,tcf->dcf", normed_second, grad_gu, preferred_element_type=jnp.float32
    )
    partial_normed = jnp.einsum(
        "tcf,dcf->td", grad_gu, full_gate_up, preferred_element_type=jnp.float32
    )
    grad_normed2 = lax.psum(partial_normed, "tp")
    mlp_gain_grad, grad_mid_norm = norm_backward(
        mid_stream, inv_second, full_mlp_gain, grad_normed2
    )
    grad_mid = grad_top.astype(jnp.float32) + grad_mid_norm
    grad_mid_b = grad_mid.astype(jnp.bfloat16)
    out_grad = jnp.einsum(
        "tk,td->kd", attended_flat, grad_mid_b, preferred_element_type=jnp.float32
    )
    grad_attended = (
        jnp.einsum("td,kd->tk", grad_mid_b, full_out, preferred_element_type=jnp.float32)
        .astype(jnp.bfloat16)
        .reshape(row_count, KV, groups, HD)
    )
    row_delta = jnp.transpose(
        jnp.sum(grad_attended.astype(jnp.float32) * attended.astype(jnp.float32), axis=-1),
        (1, 2, 0),
    )
    grad_q, grad_keys, grad_values = attention_backward(
        queries, layout, query_index, query_segs, log_norm, grad_attended, row_delta
    )
    grad_kv_all = jnp.stack([grad_keys, grad_values], axis=1).reshape(-1, 2 * KV * HD)
    grad_kv_local = lax.psum_scatter(grad_kv_all, "ctx", scatter_dimension=0, tiled=True).reshape(
        row_count, 2, KV, HD
    )
    grad_query = (
        unrotate(grad_q.reshape(row_count, H, HD), cos_table, sin_table)
        .astype(jnp.bfloat16)
        .reshape(row_count, H * HD)
    )
    grad_kv = (
        jnp.stack(
            [unrotate(grad_kv_local[:, 0], cos_table, sin_table), grad_kv_local[:, 1]], axis=1
        )
        .astype(jnp.bfloat16)
        .reshape(row_count, 2 * KV * HD)
    )
    query_grad = jnp.einsum(
        "td,tk->dk", normed_first, grad_query, preferred_element_type=jnp.float32
    )
    kv_grad = jnp.einsum("td,tk->dk", normed_first, grad_kv, preferred_element_type=jnp.float32)
    grad_normed1 = jnp.einsum(
        "tk,dk->td", grad_query, full_query, preferred_element_type=jnp.float32
    ) + jnp.einsum("tk,dk->td", grad_kv, full_kv, preferred_element_type=jnp.float32)
    attn_gain_grad, grad_in_norm = norm_backward(stream, inv_first, full_attn_gain, grad_normed1)
    input_grad = (grad_mid + grad_in_norm).reshape(1, row_count, D)
    sum_attn_gain, sum_query, sum_kv, sum_out, sum_mlp_gain, sum_gate_up, sum_down = lax.psum(
        (attn_gain_grad, query_grad, kv_grad, out_grad, mlp_gain_grad, gate_up_grad, down_grad),
        "ctx",
    )
    shard_attn_gain, shard_query, shard_kv, shard_out, shard_mlp_gain, shard_gate_up, shard_down = (
        lax.psum_scatter(sum_attn_gain, "fsdp", scatter_dimension=0, tiled=True),
        lax.psum_scatter(sum_query, "fsdp", scatter_dimension=0, tiled=True),
        lax.psum_scatter(sum_kv, "fsdp", scatter_dimension=0, tiled=True),
        lax.psum_scatter(sum_out, "fsdp", scatter_dimension=0, tiled=True),
        lax.psum_scatter(sum_mlp_gain, "fsdp", scatter_dimension=0, tiled=True),
        lax.psum_scatter(sum_gate_up, "fsdp", scatter_dimension=0, tiled=True),
        lax.psum_scatter(sum_down, "fsdp", scatter_dimension=0, tiled=True),
    )
    return (
        block_out,
        input_grad,
        shard_attn_gain,
        shard_query,
        shard_kv,
        shard_out,
        shard_mlp_gain,
        shard_gate_up,
        shard_down,
    )


def solution(mesh):
    return jax.shard_map(
        shards,
        mesh=mesh,
        in_specs=(
            P("fsdp", "ctx", None),
            P("fsdp", "ctx"),
            P("fsdp", "ctx"),
            P("fsdp"),
            P("fsdp", None),
            P("fsdp", None),
            P("fsdp", None),
            P("fsdp"),
            P("fsdp", None, "tp"),
            P("fsdp", "tp"),
            P("fsdp", "ctx", None),
        ),
        out_specs=(
            P("fsdp", "ctx", None),
            P("fsdp", "ctx", None),
            P("fsdp"),
            P("fsdp", None),
            P("fsdp", None),
            P("fsdp", None),
            P("fsdp"),
            P("fsdp", None, "tp"),
            P("fsdp", "tp"),
        ),
        check_vma=False,
    )
```

profile of v0, /device:TPU:0, one launch (start us, length us, event | category | flops | bytes accessed | tf_op | source)
XLA Modules:
  0.0 583.6 jit_solution(13312678453432094643)
XLA Ops:
  9.4 1.4 fusion.178
  13.2 5.9 %all-reduce.7 = (bf16[576]{0:T(1024)(128)(2,1)S(1)}, bf16[576]{0:T(1024)(128)(2,1)S(1)}) all-reduce(bf16[576]{0:T(1024)(128)(2,1)S(1)} %dynamic-update-slice, bf16[576]{0:T(1024)(128)(2,1)S(1)} %dynamic-update-slice.1), channel_id=1, replica_groups=mesh['fsdp'=2,'ctx'=4,'tp'=4] {'fsdp'}, use_global_device_ids=true, to_apply=%add | all-reduce | flops 1152 | bytes 4608
  19.1 7.4 %all_gather.28 = bf16[576,384]{1,0:T(8,128)(2,1)S(1)} all-gather(bf16[288,384]{1,0:T(8,128)(2,1)} %param.22), channel_id=1, replica_groups=mesh['fsdp'=2,'ctx'=4,'tp'=4] {'fsdp'}, dimensions={0}, use_global_device_ids=true | all-gather | bytes 663552 | tf_op jit(solution)/shard_map/all_gather | solution.py:235
  27.9 11.6 %all-gather = s32[1,1024]{1,0:T(1,128)S(1)} all-gather(s32[1,256]{1,0:T(1,128)} %param.18), channel_id=2, replica_groups=mesh['fsdp'=2,'ctx'=4,'tp'=4] {'ctx'}, dimensions={1}, use_global_device_ids=true | all-gather | bytes 5120 | tf_op jit(solution)/shard_map/all_gather | solution.py:260
  40.6 8.6 %all_gather.35 = bf16[576,384]{1,0:T(8,128)(2,1)} all-gather(bf16[288,384]{1,0:T(8,128)(2,1)S(1)} %copy-done.30), channel_id=1, replica_groups=mesh['fsdp'=2,'ctx'=4,'tp'=4] {'fsdp'}, dimensions={0}, use_global_device_ids=true | all-gather | bytes 663552 | tf_op jit(solution)/shard_map/all_gather | solution.py:239
  49.3 9.0 %all_gather.34 = bf16[576,2,384]{2,0,1:T(8,128)(2,1)S(1)} all-gather(bf16[288,2,384]{2,0,1:T(8,128)(2,1)S(1)} %copy.73), channel_id=1, replica_groups=mesh['fsdp'=2,'ctx'=4,'tp'=4] {'fsdp'}, dimensions={0}, use_global_device_ids=true | all-gather | bytes 1327104 | tf_op jit(solution)/shard_map/all_gather | solution.py:238
  58.6 16.2 %all_gather.29 = bf16[1024,384]{0,1:T(8,128)(2,1)S(1)} all-gather(bf16[256,384]{0,1:T(8,128)(2,1)S(1)} %bitcast.697), channel_id=1, replica_groups=mesh['fsdp'=2,'ctx'=4,'tp'=4] {'ctx'}, dimensions={0}, use_global_device_ids=true | all-gather | bytes 983040 | tf_op jit(solution)/shard_map/all_gather | solution.py:259
  75.6 11.4 %all_gather.31 = bf16[576,576]{1,0:T(8,128)(2,1)} all-gather(bf16[288,576]{1,0:T(8,128)(2,1)} %param.21), channel_id=1, replica_groups=mesh['fsdp'=2,'ctx'=4,'tp'=4] {'fsdp'}, dimensions={0}, use_global_device_ids=true | all-gather | bytes 995328 | tf_op jit(solution)/shard_map/all_gather | solution.py:234
  86.9 9.6 %all_gather.32 = bf16[576,576]{1,0:T(8,128)(2,1)} all-gather(bf16[288,576]{1,0:T(8,128)(2,1)} %param.23), channel_id=1, replica_groups=mesh['fsdp'=2,'ctx'=4,'tp'=4] {'fsdp'}, dimensions={0}, use_global_device_ids=true | all-gather | bytes 995328 | tf_op jit(solution)/shard_map/all_gather | solution.py:236
  96.5 2.3 copy.69
  98.8 1.6 fusion.148
  101.3 15.4 %while.39 = (s32[]{:T(128)}, f32[3,3,256]{2,1,0:T(4,128)S(1)}, f32[3,3,256]{2,1,0:T(4,128)S(1)}, s32[1,256]{1,0:T(1,128)}, s32[2,512]{1,0:T(2,128)S(1)}, /*index...) while((s32[]{:T(128)}, f32[3,3,256]{2,1,0:T(4,128)S(1)}, ...), condition=%wide.region_8.9_spmd.clone, body=%wide.region_1.8_spmd.clone.sunk | while | flops 158482944 | bytes 11138185 | solution.py:115
  104.1 1.3 fusion.248
  105.4 1.3 fusion.247
  106.7 1.3 fusion.246
  111.8 1.3 fusion.248
  113.1 1.3 fusion.247
  114.5 1.3 fusion.246
  116.7 17.3 %while.40 = (s32[]{:T(128)}, f32[256,3,3,64]{0,3,2,1:T(8,128)S(1)}, bf16[2,512,3,64]{1,3,2,0:T(8,128)(2,1)S(1)}, s32[1,256]{1,0:T(1,128)}, s32[2,512]{1,0:T(2,12...) while((s32[]{:T(128)}, f32[256,3,3,64]{0,3,2,1:T(8,128)S(1)}, ...), condition=%wide.region_10.11_spmd.clone, body=%wide.region_9.10_spmd.clone.sunk | while | flops 308871936 | bytes 4926655 | solution.py:141
  120.2 1.6 fusion.254
  121.8 1.6 fusion.253
  123.5 1.7 fusion.252
  128.8 1.6 fusion.254
  130.5 1.6 fusion.253
  132.1 1.7 fusion.252
  134.1 1.7 multiply_reduce_fusion.3
  137.9 1.3 convolution_bitcast_fusion.7
  139.2 2.4 convolution_convert_fusion
  141.9 30.3 %all-reduce.14.cloned.1.call-done = f32[256,576]{0,1:T(8,128)} async-done(((f32[256,576]{0,1:T(8,128)}), f32[256,576]{0,1:T(8,128)}) %all-reduce.14.cloned.1.call-update) | async-done | bytes 589840 | tf_op jit(solution)/shard_map/psum | solution.py:292
  172.2 2.0 multiply_reduce_fusion
  174.2 33.3 %all-reduce.12.cloned.1.call-done = bf16[256,576]{0,1:T(8,128)(2,1)} async-done(((bf16[256,576]{0,1:T(8,128)(2,1)}), bf16[256,576]{0,1:T(8,128)(2,1)}) %all-reduce.12.cloned.1.call-update) | async-done | bytes 294928 | tf_op jit(solution)/shard_map/psum | solution.py:278
  207.5 2.1 subtract_add_fusion
  210.7 64.2 %while.41 = (s32[]{:T(128)}, f32[256,3,3,64]{0,3,2,1:T(8,128)S(1)}, f32[2,512,3,64]{1,0,3,2:T(2,128)}, f32[2,512,3,64]{1,0,3,2:T(2,128)}, bf16[2,512,3,64]{1,3,2...) while((s32[]{:T(128)}, f32[256,3,3,64]{0,3,2,1:T(8,128)S(1)}, ...), condition=%wide.region_17.18_spmd.clone, body=%wide.region_16.17_spmd.clone.sunk | while | flops 766034688 | bytes 32253128 | solution.py:206
  214.2 1.5 fusion.282
  218.0 1.5 fusion.279
  221.8 1.5 fusion.276
  224.3 1.3 fusion.285
  226.7 8.1 %dynamic_update_slice.12 = f32[2,512,3,64]{1,0,3,2:T(2,128)} dynamic-update-slice(f32[2,512,3,64]{1,0,3,2:T(2,128)} %get-tuple-element.895, f32[1,512,3,64]{1,0,3,2:T(1,128)S(1)} %copy.106, s32[]{:T(128)S(6)} %copy.132, s32[]{:T(128)} %constant.73.clone.1..sunk.1, s32[]{:T(128)} %constant.73.clone.1..sunk.1, s32[]{:T(128)} %constant.73.clone.1..sunk.1) | dynamic-update-slice | bytes 786436 | tf_op jit(solution)/shard_map/while/body/jit(dynamic_update_index_in_dim)/dynamic_update_slice | solution.py:206
  234.7 8.1 %dynamic_update_slice.11 = f32[2,512,3,64]{1,0,3,2:T(2,128)} dynamic-update-slice(f32[2,512,3,64]{1,0,3,2:T(2,128)} %get-tuple-element.894, f32[1,512,3,64]{1,0,3,2:T(1,128)S(1)} %copy.105, s32[]{:T(128)S(6)} %copy.132, s32[]{:T(128)} %constant.73.clone.1..sunk.1, s32[]{:T(128)} %constant.73.clone.1..sunk.1, s32[]{:T(128)} %constant.73.clone.1..sunk.1) | dynamic-update-slice | bytes 786436 | tf_op jit(solution)/shard_map/while/body/jit(dynamic_update_index_in_dim)/dynamic_update_slice | solution.py:206
  246.3 1.5 fusion.282
  248.6 1.3 fusion.287
  250.1 1.5 fusion.279
  253.9 1.5 fusion.276
  256.4 1.3 fusion.285
  258.8 8.1 %dynamic_update_slice.12 = f32[2,512,3,64]{1,0,3,2:T(2,128)} dynamic-update-slice(f32[2,512,3,64]{1,0,3,2:T(2,128)} %get-tuple-element.895, f32[1,512,3,64]{1,0,3,2:T(1,128)S(1)} %copy.106, s32[]{:T(128)S(6)} %copy.132, s32[]{:T(128)} %constant.73.clone.1..sunk.1, s32[]{:T(128)} %constant.73.clone.1..sunk.1, s32[]{:T(128)} %constant.73.clone.1..sunk.1) | dynamic-update-slice | bytes 786436 | tf_op jit(solution)/shard_map/while/body/jit(dynamic_update_index_in_dim)/dynamic_update_slice | solution.py:206
  266.8 8.1 %dynamic_update_slice.11 = f32[2,512,3,64]{1,0,3,2:T(2,128)} dynamic-update-slice(f32[2,512,3,64]{1,0,3,2:T(2,128)} %get-tuple-element.894, f32[1,512,3,64]{1,0,3,2:T(1,128)S(1)} %copy.105, s32[]{:T(128)S(6)} %copy.132, s32[]{:T(128)} %constant.73.clone.1..sunk.1, s32[]{:T(128)} %constant.73.clone.1..sunk.1, s32[]{:T(128)} %constant.73.clone.1..sunk.1) | dynamic-update-slice | bytes 786436 | tf_op jit(solution)/shard_map/while/body/jit(dynamic_update_index_in_dim)/dynamic_update_slice | solution.py:206
  274.9 1.8 stack_reshape.7
  276.7 2.7 stack_reshape.6
  279.4 2.4 pad_maximum_fusion.2
  282.8 2.5 convolution_bitcast_fusion.6
  285.3 1.6 fusion.160
  287.6 1.6 fusion.152
  289.3 1.7 fusion.154
  291.1 26.4 %reduce-scatter.7.cloned.1.call-done = f32[256,384]{0,1:T(8,128)} async-done(((f32[1024,384]{0,1:T(8,128)}), f32[256,384]{0,1:T(8,128)}) %reduce-scatter.7.cloned.1.call-update) | async-done | bytes 393232 | tf_op jit(solution)/shard_map/reduce_scatter | solution.py:314
  319.4 1.3 fusion.150
  320.8 16.3 %reduce-scatter.17.cloned.1.call-done = f32[288,384]{1,0:T(8,128)} async-done(((f32[576,384]{1,0:T(8,128)}), f32[288,384]{1,0:T(8,128)}) %reduce-scatter.17.cloned.1.call-update) | async-done | bytes 442384 | tf_op jit(solution)/shard_map/reduce_scatter | solution.py:349
  337.0 27.2 %reduce-scatter.13.cloned.1.call-done = f32[288,576]{1,0:T(8,128)} async-done(((f32[576,576]{1,0:T(8,128)}), f32[288,576]{1,0:T(8,128)}) %reduce-scatter.13.cloned.1.call-update) | async-done | bytes 663568 | tf_op jit(solution)/shard_map/reduce_scatter | solution.py:346
  364.3 27.2 %reduce-scatter.9.cloned.1.call-done = f32[288,576]{1,0:T(8,128)} async-done(((f32[576,576]{1,0:T(8,128)}), f32[288,576]{1,0:T(8,128)}) %reduce-scatter.9.cloned.1.call-update) | async-done | bytes 663568 | tf_op jit(solution)/shard_map/reduce_scatter | solution.py:344
  391.5 30.6 %reduce-scatter.15.cloned.1.call-done = f32[288,2,384]{2,0,1:T(8,128)} async-done(((f32[576,2,384]{2,0,1:T(8,128)}), f32[288,2,384]{2,0,1:T(8,128)}) %reduce-scatter.15.cloned.1.call-update) | async-done | bytes 884752 | tf_op jit(solution)/shard_map/reduce_scatter | solution.py:348
  422.1 21.5 %reduce-scatter.11.cloned.1.call-done = f32[288,384]{1,0:T(8,128)} async-done(((f32[576,384]{1,0:T(8,128)}), f32[288,384]{1,0:T(8,128)}) %reduce-scatter.11.cloned.1.call-update) | async-done | bytes 442384 | tf_op jit(solution)/shard_map/reduce_scatter | solution.py:345
  445.5 5.0 all-reduce.6
  450.6 12.9 %all-reduce.4 = (f32[288]{0:T(512)}, f32[288]{0:T(512)}) all-reduce(f32[288]{0:T(512)S(1)} %dynamic-slice.3, f32[288]{0:T(512)S(1)} %dynamic-slice.5), channel_id=1, replica_groups=mesh['fsdp'=2,'ctx'=4,'tp'=4] {'ctx'}, use_global_device_ids=true, to_apply=%region_21.22 | all-reduce | flops 576 | bytes 4608 | tf_op jit(solution)/shard_map/psum | solution.py:338
  464.5 106.4 %all-reduce.16.cloned.1.call-done = (f32[288,576]{1,0:T(8,128)}, f32[288,384]{1,0:T(8,128)}, f32[288,576]{1,0:T(8,128)}, f32[288,2,384]{2,0,1:T(8,128)}, f32[288,384]{1,0:T(8,128)}) async-done(((f32[288,576]{1,0:T(8,128)}, f32[288,384]{1,0:T(8,128)}, f32[288,576]{1,0:T(8,128)}, f32[288,2,384]{2,0,1:T(8,128)}, f32[288,384]{1,0:T(8,128)}), (f32[288,576]{1,0:T(8,128)}, f32[288,384]{1,0:T(8,128)}, ...) | async-done | bytes 3096592 | tf_op jit(solution)/shard_map/psum | solution.py:338
  570.9 2.9 copy.78
  (246 shorter events, 54.5 us)
Async XLA Ops:
  7.2 19.6 %copy-start = (bf16[1,256,576]{1,2,0:T(8,128)(2,1)S(1)}, bf16[1,256,576]{1,2,0:T(8,128)(2,1)}, u32[]{:S(2)}) copy-start(bf16[1,256,576]{1,2,0:T(8,128)(2,1)} %param.17) | copy-start | bytes 884740
  7.2 165.0 %all-reduce.14.cloned.1.call-start = ((), (), s32[]{:S(2)}) async-start(), calls=%async_computation.7 | async-start | bytes 1179648 | tf_op jit(solution)/shard_map/psum | solution.py:292
  9.4 89.4 %copy-start.35 = (f32[256]{0:T(256)}, f32[256]{0:T(256)S(1)}, u32[]{:S(2)}) copy-start(f32[256]{0:T(256)S(1)} %get-tuple-element.535) | copy-start | bytes 3076
  19.1 79.7 %copy-start.31 = (f32[576]{0:T(1024)}, f32[576]{0:T(1024)S(1)}, u32[]{:S(2)}) copy-start(f32[576]{0:T(1024)S(1)} %convert_element_type.143) | copy-start | bytes 6916
  19.1 8.2 %copy-start.41 = (s32[1,256]{1,0:T(1,128)S(1)}, s32[1,256]{1,0:T(1,128)}, u32[]{:S(2)}) copy-start(s32[1,256]{1,0:T(1,128)} %param.19) | copy-start | bytes 3076
  19.1 21.6 %copy-start.30 = (bf16[288,384]{1,0:T(8,128)(2,1)S(1)}, bf16[288,384]{1,0:T(8,128)(2,1)}, u32[]{:S(2)}) copy-start(bf16[288,384]{1,0:T(8,128)(2,1)} %param.26) | copy-start | bytes 663556
  26.5 0.8 copy-start.5
  26.5 22.8 %copy-start.24 = (bf16[288,2,384]{2,1,0:T(2,128)(2,1)S(1)}, bf16[288,2,384]{2,1,0:T(2,128)(2,1)}, u32[]{:S(2)}) copy-start(bf16[288,2,384]{2,1,0:T(2,128)(2,1)} %param.25) | copy-start | bytes 1327108
  58.5 16.3 %copy-start.11 = (f32[256,32]{0,1:T(8,128)}, f32[256,32]{0,1:T(8,128)S(1)}, u32[]{:S(2)}) copy-start(f32[256,32]{0,1:T(8,128)S(1)} %get-tuple-element.532) | copy-start | bytes 98308
  58.5 16.3 %copy-start.14 = (f32[256,32]{0,1:T(8,128)}, f32[256,32]{0,1:T(8,128)S(1)}, u32[]{:S(2)}) copy-start(f32[256,32]{0,1:T(8,128)S(1)} %get-tuple-element.533) | copy-start | bytes 98308
  96.5 3.9 copy-start.12
  96.5 3.9 copy-start.15
  120.1 1.7 copy-start.7
  128.8 1.7 copy-start.7
  134.0 2.4 copy-start.33
  134.1 2.9 copy-start.8
  135.8 1.2 copy-start.27
  135.8 1.2 copy-start.28
  136.4 1.1 copy-start.37
  137.0 0.9 copy-start.21
  137.9 3.7 copy-start.17
  137.9 3.7 copy-start.19
  139.2 68.3 %all-reduce.12.cloned.1.call-start = ((), (), s32[]{:S(2)}) async-start(), calls=%async_computation.6 | async-start | bytes 589824 | tf_op jit(solution)/shard_map/psum | solution.py:278
  141.6 175.8 %reduce-scatter.7.cloned.1.call-start = ((), (), s32[]{:S(2)}) async-start(), calls=%async_computation.8 | async-start | bytes 1966080 | tf_op jit(solution)/shard_map/reduce_scatter | solution.py:314
  172.2 35.4 %copy-start.10 = (f32[256,576]{0,1:T(8,128)S(1)}, f32[256,576]{0,1:T(8,128)}, u32[]{:S(2)}) copy-start(f32[256,576]{0,1:T(8,128)} %all-reduce.14.cloned.1.call-done) | copy-start | bytes 1769476
  207.5 2.1 copy-start.3
  209.6 1.1 copy-start.1
  281.8 1.0 copy-start.29
  281.8 3.5 copy-start.2
  281.9 3.5 copy-start.9
  281.9 55.2 %reduce-scatter.17.cloned.1.call-start = ((), (), s32[]{:S(2)}) async-start(), calls=%async_computation.13 | async-start | bytes 1327104 | tf_op jit(solution)/shard_map/reduce_scatter | solution.py:349
  285.3 1.7 copy-start.13
  285.3 1.7 copy-start.16
  285.3 79.0 %reduce-scatter.13.cloned.1.call-start = ((), (), s32[]{:S(2)}) async-start(), calls=%async_computation.11 | async-start | bytes 2211840 | tf_op jit(solution)/shard_map/reduce_scatter | solution.py:346
  286.9 0.7 copy-start.32
  286.9 0.7 copy-start.36
  286.9 104.5 %reduce-scatter.9.cloned.1.call-start = ((), (), s32[]{:S(2)}) async-start(), calls=%async_computation.9 | async-start | bytes 2211840 | tf_op jit(solution)/shard_map/reduce_scatter | solution.py:344
  287.6 1.7 copy-start.18
  287.6 1.7 copy-start.20
  287.6 1.7 copy-start.34
  287.6 1.7 copy-start.38
  289.2 132.9 %reduce-scatter.15.cloned.1.call-start = ((), (), s32[]{:S(2)}) async-start(), calls=%async_computation.12 | async-start | bytes 2654208 | tf_op jit(solution)/shard_map/reduce_scatter | solution.py:348
  291.0 152.6 %reduce-scatter.11.cloned.1.call-start = ((), (), s32[]{:S(2)}) async-start(), calls=%async_computation.10 | async-start | bytes 1327104 | tf_op jit(solution)/shard_map/reduce_scatter | solution.py:345
  320.7 250.2 %all-reduce.16.cloned.1.call-start = ((), (), s32[]{:S(2)}) async-start(), calls=%async_computation.14 | async-start | bytes 6488064 | tf_op jit(solution)/shard_map/psum | solution.py:338
  443.6 1.0 copy-start.6
  443.6 1.3 copy-start.4
  444.6 0.9 copy-start.39
  444.9 18.6 %copy-start.40 = (f32[256]{0:T(256)S(1)}, f32[256]{0:T(256)}, u32[]{:S(2)}) copy-start(f32[256]{0:T(256)} %get-tuple-element.534) | copy-start | bytes 3076
  570.9 2.9 copy-start.23
  570.9 3.7 copy-start.26
  573.8 1.6 copy-start.22
  573.8 2.5 copy-start.25
Sparse Core Ops, SparseCore 0:
  139.3 32.8 all-reduce.13
  175.1 32.4 all-reduce.11
  282.0 35.4 reduce-scatter.6
  319.5 17.4 reduce-scatter.16
  339.1 25.0 reduce-scatter.12
  366.4 25.0 reduce-scatter.8
  393.7 28.3 reduce-scatter.14
  424.9 18.5 reduce-scatter.10
  446.3 124.5 all-reduce.15
where the time goes:
time: 587 us; the launch traced here: 584 us
  waiting for transfers between devices  319 us (54%)
  blocking collectives  97.5 us (17%)
  local copies, waits for them, and re-layouts  65.7 us (11%)
  matrix products  58.7 us (10%)
  other arithmetic  25.3 us (4%)
  between operations  15.9 us (3%)
    psum x1, waiting for transfers between devices, shards(): lax.psum((attn_gain_grad, query_grad, kv_grad, out_grad, mlp_gain_grad, g...  106 us
    dynamic_update_slice x8, local copies, waits for them, and re-layouts, attention_backward(): lax.scan(grad_block, jnp.zeros((row_count, KV, groups, HD), jnp.float32),...  33.8 us
    psum x1, waiting for transfers between devices, shards(): lax.psum(partial_down.astype(jnp.bfloat16), 'tp').astype(jnp.float32)  33.3 us
    reduce_scatter x1, waiting for transfers between devices, shards(): lax.psum_scatter(sum_gate_up, 'fsdp', scatter_dimension=0, tiled=True)  30.6 us
    psum x1, waiting for transfers between devices, shards(): grad_normed2 = lax.psum(partial_normed, 'tp')  30.3 us
    reduce_scatter x1, waiting for transfers between devices, shards(): lax.psum_scatter(sum_out, 'fsdp', scatter_dimension=0, tiled=True)  27.2 us
    reduce_scatter x1, waiting for transfers between devices, shards(): lax.psum_scatter(sum_query, 'fsdp', scatter_dimension=0, tiled=True)  27.2 us
    reduce_scatter x1, waiting for transfers between devices, shards(): lax.psum_scatter(grad_kv_all, 'ctx', scatter_dimension=0, tiled=True)  26.4 us
  transfers between devices with their start and end apart: 9, of which 9 were waited for; matrix products, arithmetic and copies ran while one was open for 3% of the time, Pallas kernels for 0%

commit v1 on v0

v1 whole, which is shorter than its diff:
```python
import functools

import jax
import jax.numpy as jnp
from jax import lax
from jax.experimental import pallas as pl
from jax.experimental.pallas import tpu as pltpu
from jax.sharding import PartitionSpec as P

HD = 64
eps = 1e-05
theta = 100000.0
BF = jnp.bfloat16
F32 = jnp.float32
MESH = pl.DeviceIdType.MESH
VM = pl.BlockSpec(memory_space=pltpu.VMEM)


def dot(a, b, ca, cb):
    return lax.dot_general(a, b, (((ca,), (cb,)), ((), ())), preferred_element_type=F32)


def greet(peers):
    barrier = pltpu.get_barrier_semaphore()
    for peer in peers:
        pl.semaphore_signal(barrier, inc=1, device_id=peer, device_id_type=MESH)
    pl.semaphore_wait(barrier, len(peers))


def ring(axis, count, offset):
    return lax.rem(lax.axis_index(axis) + (offset + count), count)


def remote(src, dst, send, recv, device):
    copy = pltpu.make_async_remote_copy(
        src_ref=src, dst_ref=dst, send_sem=send, recv_sem=recv,
        device_id=device, device_id_type=MESH,
    )
    copy.start()
    return copy


def local(src, dst, sem):
    copy = pltpu.make_async_copy(src, dst, sem)
    copy.start()
    return copy


def gather_parts(srcs, dsts, nf, send, recv, own):
    me = lax.axis_index("fsdp")
    remotes, locals_ = [], []
    for i, (src, dst) in enumerate(zip(srcs, dsts)):
        for o in range(1, nf):
            remotes.append(
                remote(src, dst.at[me], send.at[i, o], recv.at[i, o], {"fsdp": ring("fsdp", nf, o)})
            )
        locals_.append(local(src, dst.at[me], own.at[i]))
    return remotes, locals_


def finish(copies):
    for copy in copies:
        copy.wait()


def first_gather_kernel(nf, k, *refs):
    srcs, dsts = refs[:k], refs[k : 2 * k]
    send, recv, own = refs[2 * k :]
    greet([{"fsdp": ring("fsdp", nf, o)} for o in range(1, nf)])
    remotes, locals_ = gather_parts(srcs, dsts, nf, send, recv, own)
    finish(locals_)
    finish(remotes)


def first_gather(arrays, nf, cid):
    k = len(arrays)
    sems = pltpu.SemaphoreType.DMA
    return pl.pallas_call(
        functools.partial(first_gather_kernel, nf, k),
        out_shape=[jax.ShapeDtypeStruct((nf,) + a.shape, a.dtype) for a in arrays],
        in_specs=[VM] * k,
        out_specs=[VM] * k,
        scratch_shapes=[sems((k, nf)), sems((k, nf)), sems((k,))],
        compiler_params=pltpu.CompilerParams(collective_id=cid, has_side_effects=True),
        name="first_gather",
    )(*arrays)


def attend_kernel(nf, nz, back, heads, groups, q_ref, kv_ref, pos_ref, *refs):
    weights = refs[:3]
    kvw_ref, p_ref, att_ref = refs[3:6]
    full = refs[6:9]
    ksend, krecv, kown, wsend, wrecv, wown = refs[9:]
    rows = q_ref.shape[0]
    kvh = heads // groups
    greet(
        [{"ctx": ring("ctx", nz, o)} for o in range(1, nz)]
        + [{"fsdp": ring("fsdp", nf, o)} for o in range(1, nf)]
    )
    kcopies = [
        remote(kv_ref, kvw_ref.at[back - o], ksend.at[o], krecv.at[o], {"ctx": ring("ctx", nz, o)})
        for o in range(1, back + 1)
    ]
    kself = local(kv_ref, kvw_ref.at[back], kown)
    remotes, locals_ = gather_parts(weights, full, nf, wsend, wrecv, wown)
    kself.wait()
    finish(kcopies)
    window = (back + 1) * rows
    jj = lax.broadcasted_iota(jnp.int32, (rows, window), 1) - back * rows
    ii = lax.broadcasted_iota(jnp.int32, (rows, window), 0)
    visible = (jj <= ii) & (jj >= ii - pos_ref[...])
    bias = jnp.where(visible, 0.0, -1e30)
    kvw = kvw_ref[...].reshape(window, kv_ref.shape[1])
    outs = []
    for h in range(heads):
        g = h // groups
        key = kvw[:, g * HD : (g + 1) * HD]
        value = kvw[:, (kvh + g) * HD : (kvh + g + 1) * HD]
        s = dot(q_ref[:, h * HD : (h + 1) * HD], key, 1, 1) + bias
        e = jnp.exp(s - jnp.max(s, axis=1, keepdims=True))
        p = (e * (1.0 / jnp.sum(e, axis=1, keepdims=True))).astype(BF)
        p_ref[h] = p
        outs.append(dot(p, value, 1, 0).astype(BF))
    att_ref[...] = jnp.concatenate(outs, axis=1)
    finish(locals_)
    finish(remotes)


def attend(q, kv, pos, weights, nf, nz, back, heads, groups, cid):
    rows = q.shape[0]
    window = (back + 1) * rows
    sems = pltpu.SemaphoreType.DMA
    return pl.pallas_call(
        functools.partial(attend_kernel, nf, nz, back, heads, groups),
        out_shape=[
            jax.ShapeDtypeStruct((back + 1,) + kv.shape, BF),
            jax.ShapeDtypeStruct((heads, rows, window), BF),
            jax.ShapeDtypeStruct(q.shape, BF),
        ]
        + [jax.ShapeDtypeStruct((nf,) + a.shape, a.dtype) for a in weights],
        in_specs=[VM] * 6,
        out_specs=[VM] * 6,
        scratch_shapes=[
            sems((back + 1,)), sems((back + 1,)), sems(()),
            sems((3, nf)), sems((3, nf)), sems((3,)),
        ],
        compiler_params=pltpu.CompilerParams(collective_id=cid, has_side_effects=True),
        name="attend",
    )(q, kv, pos, *weights)


def tp_sum_kernel(nt, x_ref, out_ref, buf, piece, send, recv, gsend, grecv, own):
    me = lax.axis_index("tp")
    greet([{"tp": ring("tp", nt, o)} for o in range(1, nt)])
    copies = [
        remote(x_ref.at[ring("tp", nt, o)], buf.at[o], send.at[o], recv.at[o],
               {"tp": ring("tp", nt, o)})
        for o in range(1, nt)
    ]
    mine = local(x_ref.at[me], buf.at[0], own)
    mine.wait()
    total = buf[0].astype(F32)
    for o in range(1, nt):
        copies[o - 1].wait()
        total = total + buf[o].astype(F32)
    piece[...] = total.astype(BF)
    copies = [
        remote(piece, out_ref.at[me], gsend.at[o], grecv.at[o], {"tp": ring("tp", nt, o)})
        for o in range(1, nt)
    ]
    local(piece, out_ref.at[me], own).wait()
    finish(copies)


def tp_sum(x, nt, cid):
    sems = pltpu.SemaphoreType.DMA
    return pl.pallas_call(
        functools.partial(tp_sum_kernel, nt),
        out_shape=jax.ShapeDtypeStruct(x.shape, x.dtype),
        in_specs=[VM],
        out_specs=VM,
        scratch_shapes=[
            pltpu.VMEM(x.shape, BF), pltpu.VMEM(x.shape[1:], BF),
            sems((nt,)), sems((nt,)), sems((nt,)), sems((nt,)), sems(()),
        ],
        compiler_params=pltpu.CompilerParams(collective_id=cid, has_side_effects=True),
        name="tp_sum",
    )(x)


def grid_offsets(nf, nz):
    return [(a, b) for a in range(nf) for b in range(nz) if (a, b) != (0, 0)]


def grid_peer(nf, nz, a, b):
    return {"fsdp": ring("fsdp", nf, a), "ctx": ring("ctx", nz, b)}


def attend_back_kernel(nf, nz, back, heads, groups, *refs):
    q_ref, kvw_ref, p_ref, att_ref, go_ref, g1_ref, g2_ref = refs[:7]
    dq_ref, dkv_ref, s1_ref, s2_ref = refs[7:11]
    dw_buf, rk_buf, b1, b2, ssem, rsem, own, ksend, krecv = refs[11:]
    rows = q_ref.shape[0]
    kvh = heads // groups
    offsets = grid_offsets(nf, nz)
    greet([grid_peer(nf, nz, a, b) for a, b in offsets])
    me = lax.axis_index("fsdp") * nz + lax.axis_index("ctx")
    copies = []
    for i, (src, buf) in enumerate(((g1_ref, b1), (g2_ref, b2))):
        for a, b in offsets:
            target = ring("fsdp", nf, a) * nz + ring("ctx", nz, b)
            slot = a * nz + b
            copies.append(
                remote(src.at[target], buf.at[slot], ssem.at[i, slot], rsem.at[i, slot],
                       grid_peer(nf, nz, a, b))
            )
    mine = [local(g1_ref.at[me], b1.at[0], own.at[0]), local(g2_ref.at[me], b2.at[0], own.at[1])]
    window = (back + 1) * rows
    kvw = kvw_ref[...].reshape(window, kvw_ref.shape[2])
    dks, dvs, dqs = [], [], []
    for g in range(kvh):
        key = kvw[:, g * HD : (g + 1) * HD]
        value = kvw[:, (kvh + g) * HD : (kvh + g + 1) * HD]
        dk = jnp.zeros((window, HD), F32)
        dv = jnp.zeros((window, HD), F32)
        for h in range(g * groups, (g + 1) * groups):
            q = q_ref[:, h * HD : (h + 1) * HD]
            go = go_ref[:, h * HD : (h + 1) * HD]
            att = att_ref[:, h * HD : (h + 1) * HD]
            delta = jnp.sum(go.astype(F32) * att.astype(F32), axis=1, keepdims=True)
            p = p_ref[h]
            ds = (p.astype(F32) * (dot(go, value, 1, 1) - delta)).astype(BF)
            dv = dv + dot(p, go, 0, 0)
            dk = dk + dot(ds, q, 0, 0)
            dqs.append(dot(ds, key, 1, 0))
        dks.append(dk)
        dvs.append(dv)
    dkv = jnp.concatenate(dks + dvs, axis=1).reshape(back + 1, rows, 2 * kvh * HD)
    dw_buf[...] = dkv[:back].astype(BF)
    kcopies = [
        remote(dw_buf.at[back - o], rk_buf.at[o - 1], ksend.at[o], krecv.at[o],
               {"ctx": ring("ctx", nz, -o)})
        for o in range(1, back + 1)
    ]
    dq_ref[...] = jnp.concatenate(dqs, axis=1) * HD ** (-0.5)
    finish(mine)
    finish(kcopies)
    total = dkv[back]
    for o in range(back):
        total = total + rk_buf[o].astype(F32)
    dkv_ref[...] = total
    finish(copies)
    for buf, out in ((b1, s1_ref), (b2, s2_ref)):
        total = buf[0].astype(F32)
        for i in range(1, nf * nz):
            total = total + buf[i].astype(F32)
        out[...] = total.astype(BF)


def attend_back(q, kvw, p, att, go, g1, g2, nf, nz, back, heads, groups, cid):
    rows = q.shape[0]
    sems = pltpu.SemaphoreType.DMA
    n = nf * nz
    return pl.pallas_call(
        functools.partial(attend_back_kernel, nf, nz, back, heads, groups),
        out_shape=[
            jax.ShapeDtypeStruct(q.shape, F32),
            jax.ShapeDtypeStruct(kvw.shape[1:], F32),
            jax.ShapeDtypeStruct(g1.shape[1:], BF),
            jax.ShapeDtypeStruct(g2.shape[1:], BF),
        ],
        in_specs=[VM] * 7,
        out_specs=[VM] * 4,
        scratch_shapes=[
            pltpu.VMEM((back,) + kvw.shape[1:], BF), pltpu.VMEM((back,) + kvw.shape[1:], BF),
            pltpu.VMEM(g1.shape, BF), pltpu.VMEM(g2.shape, BF),
            sems((2, n)), sems((2, n)), sems((2,)), sems((back + 1,)), sems((back + 1,)),
        ],
        compiler_params=pltpu.CompilerParams(collective_id=cid, has_side_effects=True),
        name="attend_back",
    )(q, kvw, p, att, go, g1, g2)


def last_sum_kernel(nf, nz, nt, *refs):
    w_ref, v_ref, s1_ref, s2_ref, out_ref, vout_ref, o1_ref, o2_ref = refs[:8]
    buf, vbuf, piece, vpiece, ssem, rsem, own, gsend, grecv, tsend, trecv = refs[8:]
    offsets = grid_offsets(nf, nz)
    z = lax.axis_index("ctx")
    cols = piece.shape[1]
    columns = pl.ds(pl.multiple_of(lax.axis_index("tp") * cols, cols), cols)
    greet(
        [grid_peer(nf, nz, a, b) for a, b in offsets]
        + [{"tp": ring("tp", nt, o)} for o in range(1, nt)]
    )
    me = lax.axis_index("fsdp") * nz + z
    copies = []
    for a, b in offsets:
        target = ring("fsdp", nf, a) * nz + ring("ctx", nz, b)
        slot = a * nz + b
        peer = grid_peer(nf, nz, a, b)
        copies.append(
            remote(w_ref.at[target, :, columns], buf.at[slot], ssem.at[0, slot], rsem.at[0, slot], peer)
        )
        copies.append(
            remote(v_ref.at[target], vbuf.at[slot], ssem.at[1, slot], rsem.at[1, slot], peer)
        )
    mine = [
        local(w_ref.at[me, :, columns], buf.at[0], own.at[0]),
        local(v_ref.at[me], vbuf.at[0], own.at[1]),
        local(s1_ref, o1_ref.at[z], own.at[2]),
        local(s2_ref, o2_ref.at[z], own.at[3]),
    ]
    gathers = []
    for i, (src, dst) in enumerate(((s1_ref, o1_ref), (s2_ref, o2_ref))):
        for o in range(1, nz):
            gathers.append(
                remote(src, dst.at[z], gsend.at[i, o], grecv.at[i, o], {"ctx": ring("ctx", nz, o)})
            )
    finish(mine)
    finish(copies)
    for source, target in ((buf, piece), (vbuf, vpiece)):
        total = source[0].astype(F32)
        for i in range(1, nf * nz):
            total = total + source[i].astype(F32)
        target[...] = total.astype(target.dtype)
    late = []
    for i, (src, dst) in enumerate(
        ((piece, out_ref.at[z, :, columns]), (vpiece, vout_ref.at[z]))
    ):
        for o in range(1, nz):
            late.append(
                remote(src, dst, gsend.at[2 + i, o], grecv.at[2 + i, o], {"ctx": ring("ctx", nz, o)})
            )
        local(src, dst, own.at[i]).wait()
    finish(late)
    part = out_ref.at[:, :, columns]
    finish(
        [
            remote(part, part, tsend.at[o], trecv.at[o], {"tp": ring("tp", nt, o)})
            for o in range(1, nt)
        ]
    )
    finish(gathers)


def last_sum(w, v, s1, s2, nf, nz, nt, cid):
    sems = pltpu.SemaphoreType.DMA
    n, rows, cols = w.shape
    part = cols // nt
    return pl.pallas_call(
        functools.partial(last_sum_kernel, nf, nz, nt),
        out_shape=[
            jax.ShapeDtypeStruct((nz, rows, cols), BF),
            jax.ShapeDtypeStruct((nz,) + v.shape[1:], F32),
            jax.ShapeDtypeStruct((nz,) + s1.shape, BF),
            jax.ShapeDtypeStruct((nz,) + s2.shape, BF),
        ],
        in_specs=[VM] * 4,
        out_specs=[VM] * 4,
        scratch_shapes=[
            pltpu.VMEM((n, rows, part), BF), pltpu.VMEM(v.shape, F32),
            pltpu.VMEM((rows, part), BF), pltpu.VMEM(v.shape[1:], F32),
            sems((2, n)), sems((2, n)), sems((4,)),
            sems((4, nz)), sems((4, nz)), sems((nt,)), sems((nt,)),
        ],
        compiler_params=pltpu.CompilerParams(collective_id=cid, has_side_effects=True),
        name="last_sum",
    )(w, v, s1, s2)


def swap_halves(x):
    width = x.shape[1]
    lane = lax.broadcasted_iota(jnp.int32, x.shape, 1) % HD
    half = HD // 2
    return jnp.where(lane < half, jnp.roll(x, -half, axis=1), jnp.roll(x, half, axis=1))


def rotary(pos, count, plain):
    freq = theta ** (-2.0 * jnp.arange(HD // 2, dtype=F32) / HD)
    angles = pos.astype(F32)[:, None] * freq[None, :]
    cos, sin = jnp.cos(angles), jnp.sin(angles)
    rows = pos.shape[0]
    c = jnp.tile(jnp.concatenate([cos, cos], axis=1), (1, count))
    s = jnp.tile(jnp.concatenate([-sin, sin], axis=1), (1, count))
    return (
        jnp.concatenate([c, jnp.ones((rows, plain), F32)], axis=1),
        jnp.concatenate([s, jnp.zeros((rows, plain), F32)], axis=1),
    )


def inverse_rms(x):
    return lax.rsqrt(jnp.mean(x * x, axis=-1, keepdims=True) + eps)


def norm_back(x, inv, gain, grad):
    scaled = grad * gain
    gain_grad = jnp.sum(grad * x * inv, axis=0)
    return gain_grad, inv * scaled - x * inv**3 * jnp.mean(scaled * x, axis=-1, keepdims=True)


def shards(nf, nz, nt, hidden_in, segments, positions, attn_gain, query_weight, kv_weight,
           out_weight, mlp_gain, gate_up_weight, down_weight, cotangent):
    rows, d = hidden_in.shape[1:]
    heads = query_weight.shape[1] // HD
    kvh = kv_weight.shape[1] // (2 * HD)
    groups = heads // kvh
    dq, dkv = heads * HD, 2 * kvh * HD
    ff = down_weight.shape[1]
    span = rows * nz // 2
    back = min(nz - 1, -(-(span - 1) // rows))
    x = hidden_in.reshape(rows, d).astype(F32)
    pos = positions.reshape(rows)
    top = cotangent.reshape(rows, d)

    gains, wq, wkv = first_gather(
        [jnp.stack([attn_gain, mlp_gain]), query_weight, kv_weight], nf, 1
    )
    gains = jnp.transpose(gains, (1, 0, 2)).reshape(2, d).astype(F32)
    gain1, gain2 = gains[0], gains[1]
    wqkv = jnp.concatenate([wq.reshape(d, dq), wkv.reshape(d, dkv)], axis=1)
    ctab, stab = rotary(pos, heads + kvh, kvh * HD)
    r1 = inverse_rms(x)
    n1 = (x * r1 * gain1).astype(BF)
    raw = dot(n1, wqkv, 1, 0)
    qkv = (raw * ctab + swap_halves(raw) * stab).astype(BF)
    q = qkv[:, :dq] * jnp.asarray(HD ** (-0.5), BF)
    kv = qkv[:, dq:]

    kvw, p, att, wo, wgu, wd = attend(
        q, kv, pos[:, None],
        [out_weight, gate_up_weight.reshape(-1, 2 * ff), down_weight],
        nf, nz, back, heads, groups, 2,
    )
    wo = wo.reshape(dq, d)
    wgu = wgu.reshape(d, 2 * ff)
    wd = wd.reshape(d, ff)
    mid = x + dot(att, wo, 1, 0)
    r2 = inverse_rms(mid)
    n2 = (mid * r2 * gain2).astype(BF)
    gu = dot(n2, wgu, 1, 0)
    gate, up = gu[:, :ff], gu[:, ff:]
    sig = jax.nn.sigmoid(gate)
    hidden = (gate * sig * up).astype(BF)
    gh = dot(top, wd, 1, 0)
    ggu = jnp.concatenate(
        [gh * up * sig * (1.0 + gate * (1.0 - sig)), gh * gate * sig], axis=1
    ).astype(BF)
    part = jnp.concatenate([dot(hidden, wd, 1, 1), dot(ggu, wgu, 1, 1)], axis=1).astype(BF)
    summed = tp_sum(part.reshape(nt, rows // nt, 2 * d), nt, 3).reshape(rows, 2 * d).astype(F32)
    block_out = (mid + summed[:, :d]).astype(BF).reshape(1, rows, d)
    n = nf * nz
    down_grad = dot(top, hidden, 0, 0).astype(BF).reshape(n, d // n, ff)
    gu_grad = dot(n2, ggu, 0, 0).astype(BF).reshape(n, d // n, 2 * ff)
    mlp_gain_grad, grad_norm = norm_back(mid, r2, gain2, summed[:, d:])
    grad_mid = top.astype(F32) + grad_norm
    grad_mid_b = grad_mid.astype(BF)
    go = dot(grad_mid_b, wo, 1, 1).astype(BF)

    grad_q, grad_kv, s1, s2 = attend_back(
        q, kvw, p, att, go, gu_grad, down_grad, nf, nz, back, heads, groups, 4
    )
    grads = jnp.concatenate([grad_q, grad_kv], axis=1)
    grads = (grads * ctab - swap_halves(grads) * stab).astype(BF)
    dw = jnp.concatenate([dot(n1, grads, 0, 0), dot(att, grad_mid_b, 0, 0)], axis=1)
    grad_n1 = dot(grads, wqkv, 1, 1)
    attn_gain_grad, grad_in = norm_back(x, r1, gain1, grad_n1)
    input_grad = (grad_mid + grad_in).reshape(1, rows, d)
    gain_grads = jnp.transpose(
        jnp.stack([attn_gain_grad, mlp_gain_grad]).reshape(2, n, d // n), (1, 0, 2)
    )
    out, gout, o1, o2 = last_sum(
        dw.astype(BF).reshape(n, d // n, -1), gain_grads, s1, s2, nf, nz, nt, 5
    )
    local_d = d // nf
    out = out.reshape(local_d, -1).astype(F32)
    gout = jnp.transpose(gout, (1, 0, 2)).reshape(2, local_d)
    return (
        block_out,
        input_grad,
        gout[0],
        out[:, :dq],
        out[:, dq : dq + dkv],
        out[:, dq + dkv :],
        gout[1],
        o1.reshape(local_d, 2, ff).astype(F32),
        o2.reshape(local_d, ff).astype(F32),
    )


def solution(mesh):
    sizes = mesh.shape
    return jax.shard_map(
        functools.partial(shards, sizes["fsdp"], sizes["ctx"], sizes["tp"]),
        mesh=mesh,
        in_specs=(
            P("fsdp", "ctx", None), P("fsdp", "ctx"), P("fsdp", "ctx"), P("fsdp"),
            P("fsdp", None), P("fsdp", None), P("fsdp", None), P("fsdp"),
            P("fsdp", None, "tp"), P("fsdp", "tp"), P("fsdp", "ctx", None),
        ),
        out_specs=(
            P("fsdp", "ctx", None), P("fsdp", "ctx", None), P("fsdp"),
            P("fsdp", None), P("fsdp", None), P("fsdp", None), P("fsdp"),
            P("fsdp", None, "tp"), P("fsdp", "tp"),
        ),
        check_vma=False,
    )
```

time: 587 us -> 217 us (0.37)
  waiting for transfers between devices: 319 us -> 0 us
  Pallas kernels: 0 us -> 163 us
  blocking collectives: 97.5 us -> 0 us
  local copies, waits for them, and re-layouts: 65.7 us -> 19.1 us
  matrix products: 58.7 us -> 12.4 us
  between operations: 15.9 us -> 1.18 us
    psum x3 -> x0, waiting for transfers between devices: 170 us -> none  [the longest x1 106 us: shards(): lax.psum((attn_gain_grad, query_grad, kv_grad, out_grad, mlp_gain_grad, g...]
    pallas_call x0 -> x5, Pallas kernels: none -> 163 us  [the longest x1 49.9 us: attend_back(): pl.pallas_call(functools.partial(attend_back_kernel, nf, nz, back, heads,...]
    reduce_scatter x6 -> x0, waiting for transfers between devices: 149 us -> none  [the longest x1 30.6 us: shards(): lax.psum_scatter(sum_gate_up, 'fsdp', scatter_dimension=0, tiled=True)]
    all_gather x7 -> x0, blocking collectives: 73.7 us -> none  [the longest x1 16.2 us: shards(): kv_all = lax.all_gather(kv_local, 'ctx', axis=0, tiled=True)]
    dot_general x57 -> x12, matrix products: 58.7 us -> 12.4 us  [dot(): lax.dot_general(a, b, (((ca,), (cb,)), ((), ())), preferred_element_type=...]
    dynamic_update_slice x8 -> x0, local copies, waits for them, and re-layouts: 33.8 us -> none  [attention_backward(): lax.scan(grad_block, jnp.zeros((row_count, KV, groups, HD), jnp.float32),...]
    psum x1 -> x0, blocking collectives: 12.9 us -> none  [shards(): lax.psum((attn_gain_grad, query_grad, kv_grad, out_grad, mlp_gain_grad, g...]
    unnamed x2 -> x0, blocking collectives: 10.9 us -> none
  transfers between devices with their start and end apart: 9 -> 0, of which waited for: 9 -> 0; matrix products, arithmetic and copies ran while one was open for 3% -> 0% of each run, Pallas kernels for 0% -> 0%
where the time goes in v1:
time: 217 us; the launch traced here: 216 us
  Pallas kernels  163 us (75%)
  other arithmetic  20.1 us (9%)
  local copies, waits for them, and re-layouts  19.1 us (9%)
  matrix products  12.4 us (6%)
    pallas_call x1, Pallas kernels, attend_back(): pl.pallas_call(functools.partial(attend_back_kernel, nf, nz, back, heads,...  49.9 us
    pallas_call x1, Pallas kernels, last_sum(): pl.pallas_call(functools.partial(last_sum_kernel, nf, nz, nt), out_shape=...  45.6 us
    pallas_call x1, Pallas kernels, attend(): pl.pallas_call(functools.partial(attend_kernel, nf, nz, back, heads, grou...  31.5 us
    pallas_call x1, Pallas kernels, first_gather(): pl.pallas_call(functools.partial(first_gather_kernel, nf, k), out_shape=[...  18.6 us
    pallas_call x1, Pallas kernels, tp_sum(): pl.pallas_call(functools.partial(tp_sum_kernel, nt), out_shape=jax.ShapeD...  17.7 us
    dot_general x12, matrix products, dot(): lax.dot_general(a, b, (((ca,), (cb,)), ((), ())), preferred_element_type=...  12.4 us
    unnamed x59, local copies, waits for them, and re-layouts  5.66 us

profile of v1, /device:TPU:0, one launch (start us, length us, event | category | flops | bytes accessed | tf_op | source)
XLA Modules:
  0.0 216.0 jit_solution(18322675873907141872)
XLA Ops:
  0.6 0.7 stack.19
  1.3 0.7 stack.18
  2.0 0.6 pad_maximum_fusion.8.refs_0_
  2.6 18.6 %first_gather.1 = (bf16[2,2,288]{2,1,0:T(2,128)(2,1)}, bf16[2,288,576]{2,1,0:T(8,128)(2,1)}, bf16[2,288,384]{2,1,0:T(8,128)(2,1)}) custom-call(bf16[2,288]{1,0:T(2,128)(2,1)} %pad_maximum_fusion.8.refs_0_, bf16[288,576]{1,0:T(8,128)(2,1)} %refs_1_.1, bf16[288,384]{1,0:T(8,128)(2,1)} %refs_2_.2), custom_call_target="tpu_custom_call" | custom-call | tf_op jit(solution)/shard_map/first_gather/pallas_call | solution.py:78
  21.2 0.7 convert_bitcast_fusion
  21.9 1.1 fusion.8
  23.0 0.6 multiply_multiply_fusion
  23.6 1.1 fusion.10
  24.7 2.0 fusion.7
  26.8 0.2 fusion.30
  27.1 0.3 copy.40
  27.5 0.3 copy.46
  27.7 0.1 fusion.42
  27.8 0.4 fusion.43
  28.3 0.6 fusion.1
  28.9 0.8 slice_multiply_fusion.q_ref.refs_0_
  29.6 0.8 slice.100.kv_ref
  30.5 0.8 copy.47.pos_ref
  31.3 0.8 copy.57
  32.1 31.5 %attend.1 = (bf16[3,256,384]{2,1,0:T(8,128)(2,1)}, bf16[9,256,768]{2,1,0:T(8,128)(2,1)}, bf16[256,576]{1,0:T(8,128)(2,1)}, bf16[2,288,576]{2,1,0:T(8,128)(2,1)},...) custom-call(bf16[256,576]{1,0:T(8,128)(2,1)} %slice_multiply_fusion.q_ref.refs_0_, ...), custom_call_target="tpu_custom_call" | custom-call | tf_op jit(solution)/shard_map/attend/pallas_call | solution.py:133
  63.7 1.8 multiply_reduce_fusion.2
  65.5 0.6 multiply_multiply_fusion.1
  66.1 1.8 fusion.39
  67.9 0.5 multiply_convert_fusion.2
  68.4 0.6 copy-done.10
  69.0 0.5 convolution_convert_fusion.4
  69.5 0.4 convolution_convert_fusion.5
  69.9 1.0 pad_maximum_fusion.5.x_ref
  70.9 17.7 %tp_sum.1 = bf16[4,64,1152]{2,1,0:T(8,128)(2,1)} custom-call(bf16[4,64,1152]{2,1,0:T(8,128)(2,1)} %pad_maximum_fusion.5.x_ref), custom_call_target="tpu_custom_call" | custom-call | tf_op jit(solution)/shard_map/tp_sum/pallas_call | solution.py:177
  88.6 1.1 bitcast_convert_fusion.1
  89.8 1.2 fusion.41
  91.0 1.3 copy.56
  92.3 0.9 multiply_reduce_fusion
  93.2 0.6 broadcast_multiply_fusion.1
  93.8 2.1 copy.55
  95.9 2.2 subtract_add_fusion
  98.0 0.4 convolution_convert_fusion.6
  98.4 0.9 copy.50.refs_4_
  99.3 2.4 %convolution_convert_fusion.1 = bf16[576,768]{1,0:T(8,128)(2,1)} fusion(bf16[256,384]{1,0:T(8,128)(2,1)} %copy-done.16, bf16[256,384]{1,0:T(8,128)(2,1)} %copy-done.15, f32[256,576]{0,1:T(8,128)S(1)} %get-tuple-element.74, f32[576]{0:T(1024)S(1)} %mul.196, f32[256]{0:T(256)} %copy-done.17), kind=kOutput, calls=%fused_computation.5 | convolution fusion | flops 228163584 | bytes 1871104 | tf_op jit(solution)/shard_map/dot_general | solution.py:20
  101.7 1.1 convolution_convert_fusion.3
  102.8 49.9 %attend_back.1 = (f32[256,576]{1,0:T(8,128)}, f32[256,384]{1,0:T(8,128)}, bf16[72,768]{1,0:T(8,128)(2,1)}, bf16[72,384]{1,0:T(8,128)(2,1)}) custom-call(bf16[256,576]{1,0:T(8,128)(2,1)} %slice_multiply_fusion.q_ref.refs_0_, bf16[3,256,384]{2,1,0:T(8,128)(2,1)} %get-tuple-element.33.refs_1_, bf16[9,256,768]{2,1,0:T(8,128)(2,1)} %get-tuple-element.34.refs_2_, ...), custom_call_target="tpu_custom_call" | custom-call | tf_op jit(solution)/shard_map/attend_back/pallas_call | solution.py:264
  152.8 1.0 slice.86
  153.8 2.1 fusion.5
  155.9 0.1 slice.87
  156.0 0.6 fusion.3
  156.6 0.3 copy-done.1
  156.9 0.3 copy-done.26
  157.2 0.1 copy-done.27
  157.3 0.6 fusion.17
  158.0 1.0 fusion.14
  159.0 0.5 convolution_convert_fusion.2
  159.5 0.5 convolution_convert_fusion
  160.0 1.7 pad_maximum_fusion.refs_0_
  161.7 0.1 stack.21
  161.8 0.6 maximum_bitcast_fusion.refs_1_
  162.4 45.6 %last_sum.1 = (bf16[4,72,1536]{2,1,0:T(8,128)(2,1)}, f32[4,2,72]{2,1,0:T(2,128)}, bf16[4,72,768]{2,1,0:T(8,128)(2,1)}, bf16[4,72,384]{2,1,0:T(8,128)(2,1)}) custom-call(bf16[8,72,1536]{2,1,0:T(8,128)(2,1)} %pad_maximum_fusion.refs_0_, f32[8,2,72]{2,1,0:T(2,128)} %maximum_bitcast_fusion.refs_1_, bf16[72,768]{1,0:T(8,128)(2,1)} %get-tuple-element.37.refs_2_, ...), custom_call_target="tpu_custom_call" | custom-call | tf_op jit(solution)/shard_map/last_sum/pallas_call | solution.py:350
  208.0 0.8 slice_reduce_fusion.2
  208.8 0.7 squeeze.6
  209.5 1.4 bitcast_convert_fusion
  210.8 1.3 fusion.40
  212.2 0.9 slice.112
  213.1 0.7 squeeze.7
  213.8 1.4 reshape.169
  215.2 0.8 bitcast_convert_fusion.2
  (64 shorter events, 0.6 us)
Async XLA Ops:
  23.6 3.2 %copy-start.20 = (f32[256]{0:T(256)}, f32[256]{0:T(256)S(1)}, u32[]{:S(2)}) copy-start(f32[256]{0:T(256)S(1)} %get-tuple-element.70) | copy-start | bytes 3076
  23.6 3.2 %copy-start.25 = (s32[1,256]{1,0:T(1,128)S(1)}, s32[1,256]{1,0:T(1,128)}, u32[]{:S(2)}) copy-start(s32[1,256]{1,0:T(1,128)} %param.12) | copy-start | bytes 3076
  24.7 2.4 %copy-start.8 = (bf16[256,576]{0,1:T(8,128)(2,1)}, bf16[256,576]{0,1:T(8,128)(2,1)S(1)}, u32[]{:S(2)}) copy-start(bf16[256,576]{0,1:T(8,128)(2,1)S(1)} %fusion.10) | copy-start | bytes 884740
  28.2 0.6 copy-start.22
  28.2 3.0 %copy-start.11 = (bf16[288,2,384]{2,1,0:T(2,128)(2,1)S(1)}, bf16[288,2,384]{2,1,0:T(2,128)(2,1)}, u32[]{:S(2)}) copy-start(bf16[288,2,384]{2,1,0:T(2,128)(2,1)} %param.18) | copy-start | bytes 1327108
  28.9 34.8 %copy-start = (bf16[1,256,576]{1,2,0:T(8,128)(2,1)S(1)}, bf16[1,256,576]{1,2,0:T(8,128)(2,1)}, u32[]{:S(2)}) copy-start(bf16[1,256,576]{1,2,0:T(8,128)(2,1)} %param.11) | copy-start | bytes 884740
  63.6 4.2 %copy-start.6 = (bf16[1,256,576]{1,2,0:T(8,128)(2,1)S(1)}, bf16[1,256,576]{1,2,0:T(8,128)(2,1)}, u32[]{:S(2)}) copy-start(bf16[1,256,576]{1,2,0:T(8,128)(2,1)} %param.20) | copy-start | bytes 884740
  63.6 4.2 %copy-start.12 = (bf16[2,288,384]{2,1,0:T(8,128)(2,1)S(1)}, bf16[2,288,384]{2,1,0:T(8,128)(2,1)}, u32[]{:S(2)}) copy-start(bf16[2,288,384]{2,1,0:T(8,128)(2,1)} %get-tuple-element.32) | copy-start | bytes 1327108
  66.1 2.3 %copy-start.17 = (f32[256]{0:T(256)}, f32[256]{0:T(256)S(1)}, u32[]{:S(2)}) copy-start(f32[256]{0:T(256)S(1)} %get-tuple-element.72) | copy-start | bytes 3076
  67.9 1.2 copy-start.10
  68.4 1.5 copy-start.15
  68.4 1.5 copy-start.16
  89.7 2.6 %copy-start.18 = (f32[256]{0:T(256)S(1)}, f32[256]{0:T(256)}, u32[]{:S(2)}) copy-start(f32[256]{0:T(256)} %copy-done.17) | copy-start | bytes 3076
  95.9 2.2 %copy-start.4 = (bf16[2,288,576]{2,1,0:T(8,128)(2,1)S(1)}, bf16[2,288,576]{2,1,0:T(8,128)(2,1)}, u32[]{:S(2)}) copy-start(bf16[2,288,576]{2,1,0:T(8,128)(2,1)} %get-tuple-element.30) | copy-start | bytes 1990660
  98.0 3.7 %copy-start.7 = (bf16[1,256,576]{1,2,0:T(8,128)(2,1)S(1)}, bf16[1,256,576]{1,2,0:T(8,128)(2,1)}, u32[]{:S(2)}) copy-start(bf16[1,256,576]{1,2,0:T(8,128)(2,1)} %param.20) | copy-start | bytes 884740
  152.8 3.1 %copy-start.5 = (f32[256,384]{1,0:T(8,128)S(1)}, f32[256,384]{1,0:T(8,128)}, u32[]{:S(2)}) copy-start(f32[256,384]{1,0:T(8,128)} %get-tuple-element.36) | copy-start | bytes 1179652
  153.7 2.2 %copy-start.2 = (f32[256,576]{1,0:T(8,128)S(1)}, f32[256,576]{1,0:T(8,128)}, u32[]{:S(2)}) copy-start(f32[256,576]{1,0:T(8,128)} %get-tuple-element.35) | copy-start | bytes 1769476
  153.7 2.2 %copy-start.23 = (pred[960]{0:T(1024)(128)(4,1)S(1)}, pred[960]{0:T(1024)(128)(4,1)}, u32[]{:S(2)}) copy-start(pred[960]{0:T(1024)(128)(4,1)} %copy-done.22) | copy-start | bytes 2884
  156.0 1.0 copy-start.1
  156.0 1.0 copy-start.21
  156.0 1.2 copy-start.26
  156.0 1.3 copy-start.27
  157.3 0.7 copy-start.24
  157.9 1.0 copy-start.3
  158.0 1.5 copy-start.9
  159.9 1.7 copy-start.19
  210.8 3.0 %copy-start.13 = (bf16[4,72,768]{2,1,0:T(8,128)(2,1)S(1)}, bf16[4,72,768]{2,1,0:T(8,128)(2,1)}, u32[]{:S(2)}) copy-start(bf16[4,72,768]{2,1,0:T(8,128)(2,1)} %get-tuple-element.41) | copy-start | bytes 1327108
  212.2 3.0 %copy-start.14 = (bf16[4,72,384]{2,1,0:T(8,128)(2,1)S(1)}, bf16[4,72,384]{2,1,0:T(8,128)(2,1)}, u32[]{:S(2)}) copy-start(bf16[4,72,384]{2,1,0:T(8,128)(2,1)} %get-tuple-element.42) | copy-start | bytes 663556

commit v2 on v1

--- a/solution.py
+++ b/solution.py
@@ -46,73 +46,115 @@
     return copy
 
 
-def gather_parts(srcs, dsts, nf, send, recv, own):
-    me = lax.axis_index("fsdp")
-    remotes, locals_ = [], []
-    for i, (src, dst) in enumerate(zip(srcs, dsts)):
-        for o in range(1, nf):
-            remotes.append(
-                remote(src, dst.at[me], send.at[i, o], recv.at[i, o], {"fsdp": ring("fsdp", nf, o)})
-            )
-        locals_.append(local(src, dst.at[me], own.at[i]))
-    return remotes, locals_
-
-
 def finish(copies):
     for copy in copies:
         copy.wait()
 
 
-def first_gather_kernel(nf, k, *refs):
-    srcs, dsts = refs[:k], refs[k : 2 * k]
-    send, recv, own = refs[2 * k :]
-    greet([{"fsdp": ring("fsdp", nf, o)} for o in range(1, nf)])
-    remotes, locals_ = gather_parts(srcs, dsts, nf, send, recv, own)
-    finish(locals_)
-    finish(remotes)
-
-
-def first_gather(arrays, nf, cid):
-    k = len(arrays)
-    sems = pltpu.SemaphoreType.DMA
-    return pl.pallas_call(
-        functools.partial(first_gather_kernel, nf, k),
-        out_shape=[jax.ShapeDtypeStruct((nf,) + a.shape, a.dtype) for a in arrays],
-        in_specs=[VM] * k,
-        out_specs=[VM] * k,
-        scratch_shapes=[sems((k, nf)), sems((k, nf)), sems((k,))],
-        compiler_params=pltpu.CompilerParams(collective_id=cid, has_side_effects=True),
-        name="first_gather",
-    )(*arrays)
-
-
-def attend_kernel(nf, nz, back, heads, groups, q_ref, kv_ref, pos_ref, *refs):
-    weights = refs[:3]
-    kvw_ref, p_ref, att_ref = refs[3:6]
-    full = refs[6:9]
-    ksend, krecv, kown, wsend, wrecv, wown = refs[9:]
-    rows = q_ref.shape[0]
-    kvh = heads // groups
+def across(nt):
+    return [{"tp": ring("tp", nt, o)} for o in range(1, nt)]
+
+
+def partner():
+    t = lax.axis_index("tp")
+    return {"tp": t + 1 - 2 * lax.rem(t, 2)}
+
+
+def attend_kernel(nf, nz, nt, back, heads, kvh, head_cols, *refs):
+    x_ref, pos_ref, c_ref, s_ref, gain_ref, w_ref, gu_ref, dn_ref = refs[:8]
+    n1_ref, q_ref, kvw_ref, p_ref, att_ref, fgain, fw, fgu, fdn = refs[8:17]
+    ysend, yrecv, own, psend, precv, ksend, krecv, fsend, frecv = refs[17:]
+    rows, d = x_ref.shape
+    dq, dkv, dk = heads * HD, 2 * kvh * HD, kvh * HD
+    groups = heads // kvh
+    f = lax.axis_index("fsdp")
+    core = lax.rem(lax.axis_index("tp"), 2)
+    mate = partner()
     greet(
         [{"ctx": ring("ctx", nz, o)} for o in range(1, nz)]
         + [{"fsdp": ring("fsdp", nf, o)} for o in range(1, nf)]
-    )
+        + [mate]
+    )
+    h1 = head_cols // 2
+    h2 = (w_ref.shape[1] - head_cols) // 2
+    first = pl.ds(pl.multiple_of(core * h1, 128), h1)
+    second = pl.ds(pl.multiple_of(head_cols + core * h2, 128), h2)
+    plans = [
+        (gain_ref, fgain.at[f]),
+        (w_ref.at[:, first], fw.at[f, :, first]),
+        (w_ref.at[:, second], fw.at[f, :, second]),
+        (dn_ref, fdn.at[f]),
+        (gu_ref, fgu.at[f]),
+    ]
+    sent = [
+        [
+            remote(src, dst, ysend.at[i, o], yrecv.at[i, o], {"fsdp": ring("fsdp", nf, o)})
+            for o in range(1, nf)
+        ]
+        for i, (src, dst) in enumerate(plans)
+    ]
+    mine = [
+        local(src, dst.at[f], own.at[i])
+        for i, (src, dst) in enumerate(
+            ((gain_ref, fgain), (w_ref, fw), (dn_ref, fdn), (gu_ref, fgu))
+        )
+    ]
+
+    def pass_on(i, k, columns):
+        out = []
+        for o in range(1, nf):
+            sent[i][o - 1].wait()
+            part = fw.at[ring("fsdp", nf, -o), :, columns]
+            out.append(remote(part, part, psend.at[k, o], precv.at[k, o], mate))
+        return out
+
+    x = x_ref[...].astype(F32)
+    normed = x * lax.rsqrt(jnp.mean(x * x, axis=1, keepdims=True) + eps)
+    r = lax.broadcasted_iota(jnp.int32, (dq, dq), 0)
+    c = lax.broadcasted_iota(jnp.int32, (dq, dq), 1)
+    half = HD // 2
+    lane = lax.rem(c, HD)
+    perm = jnp.where(r == jnp.where(lane < half, c + half, c - half), 1.0, 0.0).astype(BF)
+    finish(mine)
+    finish(sent[0])
+    finish(pass_on(1, 0, first))
+    gain = jnp.concatenate([fgain[i, 0:1, :] for i in range(nf)], axis=1).astype(F32)
+    n1 = (normed * gain).astype(BF)
+    n1_ref[...] = n1
+    w = fw[:, :, : dq + dkv].reshape(d, dq + dkv)
+    wq, wk = w[:, :dq], w[:, dq : dq + dk]
+    ct, st = c_ref[...], s_ref[...]
+    k = dot(n1, wk, 1, 0) * ct[:, :dk] + dot(
+        n1, dot(wk, perm[:dk, :dk], 1, 0).astype(BF), 1, 0
+    ) * st[:, :dk]
+    v = dot(n1, w[:, dq + dk :], 1, 0)
+    kvw_ref[back] = jnp.concatenate([k, v], axis=1).astype(BF)
+    hr = rows // 2
+    block = pl.ds(pl.multiple_of(core * hr, hr), hr)
     kcopies = [
-        remote(kv_ref, kvw_ref.at[back - o], ksend.at[o], krecv.at[o], {"ctx": ring("ctx", nz, o)})
+        remote(kvw_ref.at[back, block], kvw_ref.at[back - o, block], ksend.at[o], krecv.at[o],
+               {"ctx": ring("ctx", nz, o)})
         for o in range(1, back + 1)
     ]
-    kself = local(kv_ref, kvw_ref.at[back], kown)
-    remotes, locals_ = gather_parts(weights, full, nf, wsend, wrecv, wown)
-    kself.wait()
-    finish(kcopies)
+    q = dot(n1, wq, 1, 0) * ct + dot(n1, dot(wq, perm, 1, 0).astype(BF), 1, 0) * st
+    q_ref[...] = (q.astype(BF).astype(F32) * HD ** (-0.5)).astype(BF)
     window = (back + 1) * rows
     jj = lax.broadcasted_iota(jnp.int32, (rows, window), 1) - back * rows
     ii = lax.broadcasted_iota(jnp.int32, (rows, window), 0)
     visible = (jj <= ii) & (jj >= ii - pos_ref[...])
     bias = jnp.where(visible, 0.0, -1e30)
-    kvw = kvw_ref[...].reshape(window, kv_ref.shape[1])
+    shared = []
+    for o in range(1, back + 1):
+        kcopies[o - 1].wait()
+        part = kvw_ref.at[back - o, block]
+        shared.append(remote(part, part, fsend.at[o], frecv.at[o], mate))
+    finish(shared)
+    kvw = kvw_ref[...].reshape(window, dkv)
     outs = []
+    late = []
     for h in range(heads):
+        if h == heads // 2:
+            late = pass_on(2, 1, second)
         g = h // groups
         key = kvw[:, g * HD : (g + 1) * HD]
         value = kvw[:, (kvh + g) * HD : (kvh + g + 1) * HD]
@@ -122,44 +164,54 @@
         p_ref[h] = p
         outs.append(dot(p, value, 1, 0).astype(BF))
     att_ref[...] = jnp.concatenate(outs, axis=1)
-    finish(locals_)
-    finish(remotes)
-
-
-def attend(q, kv, pos, weights, nf, nz, back, heads, groups, cid):
-    rows = q.shape[0]
+    finish(late)
+    finish(sent[3])
+    finish(sent[4])
+
+
+def attend(x, pos, ct, st, gains, w, gu, dn, nf, nz, nt, back, heads, kvh, head_cols, cid):
+    rows, d = x.shape
     window = (back + 1) * rows
     sems = pltpu.SemaphoreType.DMA
+    shape = jax.ShapeDtypeStruct
     return pl.pallas_call(
-        functools.partial(attend_kernel, nf, nz, back, heads, groups),
+        functools.partial(attend_kernel, nf, nz, nt, back, heads, kvh, head_cols),
         out_shape=[
-            jax.ShapeDtypeStruct((back + 1,) + kv.shape, BF),
-            jax.ShapeDtypeStruct((heads, rows, window), BF),
-            jax.ShapeDtypeStruct(q.shape, BF),
+            shape((rows, d), BF),
+            shape((rows, heads * HD), BF),
+            shape((back + 1, rows, 2 * kvh * HD), BF),
+            shape((heads, rows, window), BF),
+            shape((rows, heads * HD), BF),
         ]
-        + [jax.ShapeDtypeStruct((nf,) + a.shape, a.dtype) for a in weights],
-        in_specs=[VM] * 6,
-        out_specs=[VM] * 6,
+        + [shape((nf,) + a.shape, a.dtype) for a in (gains, w, gu, dn)],
+        in_specs=[VM] * 8,
+        out_specs=[VM] * 9,
         scratch_shapes=[
-            sems((back + 1,)), sems((back + 1,)), sems(()),
-            sems((3, nf)), sems((3, nf)), sems((3,)),
+            sems((5, nf)), sems((5, nf)), sems((4,)), sems((2, nf)), sems((2, nf)),
+            sems((back + 1,)), sems((back + 1,)), sems((back + 1,)), sems((back + 1,)),
         ],
         compiler_params=pltpu.CompilerParams(collective_id=cid, has_side_effects=True),
         name="attend",
-    )(q, kv, pos, *weights)
-
-
-def tp_sum_kernel(nt, x_ref, out_ref, buf, piece, send, recv, gsend, grecv, own):
+    )(x, pos, ct, st, gains, w, gu, dn)
+
+
+def tp_sum_kernel(nf, nt, x_ref, g1_ref, g2_ref, out_ref, o1_ref, o2_ref, buf, piece, b1, b2,
+                  send, recv, gsend, grecv, own, ysend, yrecv):
     me = lax.axis_index("tp")
-    greet([{"tp": ring("tp", nt, o)} for o in range(1, nt)])
+    f = lax.axis_index("fsdp")
+    greet(across(nt) + [{"fsdp": ring("fsdp", nf, o)} for o in range(1, nf)])
     copies = [
         remote(x_ref.at[ring("tp", nt, o)], buf.at[o], send.at[o], recv.at[o],
                {"tp": ring("tp", nt, o)})
         for o in range(1, nt)
     ]
-    mine = local(x_ref.at[me], buf.at[0], own)
-    mine.wait()
-    total = buf[0].astype(F32)
+    side = [
+        remote(src.at[ring("fsdp", nf, o)], dst.at[o], ysend.at[i, o], yrecv.at[i, o],
+               {"fsdp": ring("fsdp", nf, o)})
+        for i, (src, dst) in enumerate(((g1_ref, b1), (g2_ref, b2)))
+        for o in range(1, nf)
+    ]
+    total = x_ref[me].astype(F32)
     for o in range(1, nt):
         copies[o - 1].wait()
         total = total + buf[o].astype(F32)
@@ -169,23 +221,32 @@
         for o in range(1, nt)
     ]
     local(piece, out_ref.at[me], own).wait()
+    finish(side)
+    for src, dst, out in ((g1_ref, b1, o1_ref), (g2_ref, b2, o2_ref)):
+        total = src[f].astype(F32)
+        for o in range(1, nf):
+            total = total + dst[o].astype(F32)
+        out[...] = total.astype(BF)
     finish(copies)
 
 
-def tp_sum(x, nt, cid):
+def tp_sum(x, g1, g2, nf, nt, cid):
     sems = pltpu.SemaphoreType.DMA
+    shape = jax.ShapeDtypeStruct
     return pl.pallas_call(
-        functools.partial(tp_sum_kernel, nt),
-        out_shape=jax.ShapeDtypeStruct(x.shape, x.dtype),
-        in_specs=[VM],
-        out_specs=VM,
+        functools.partial(tp_sum_kernel, nf, nt),
+        out_shape=[shape(x.shape, BF), shape(g1.shape[1:], BF), shape(g2.shape[1:], BF)],
+        in_specs=[VM] * 3,
+        out_specs=[VM] * 3,
         scratch_shapes=[
             pltpu.VMEM(x.shape, BF), pltpu.VMEM(x.shape[1:], BF),
+            pltpu.VMEM(g1.shape, BF), pltpu.VMEM(g2.shape, BF),
             sems((nt,)), sems((nt,)), sems((nt,)), sems((nt,)), sems(()),
+            sems((2, nf)), sems((2, nf)),
         ],
         compiler_params=pltpu.CompilerParams(collective_id=cid, has_side_effects=True),
         name="tp_sum",
-    )(x)
+    )(x, g1, g2)
 
 
 def grid_offsets(nf, nz):
@@ -196,25 +257,20 @@
     return {"fsdp": ring("fsdp", nf, a), "ctx": ring("ctx", nz, b)}
 
 
-def attend_back_kernel(nf, nz, back, heads, groups, *refs):
+def attend_back_kernel(nz, nt, back, heads, groups, *refs):
     q_ref, kvw_ref, p_ref, att_ref, go_ref, g1_ref, g2_ref = refs[:7]
     dq_ref, dkv_ref, s1_ref, s2_ref = refs[7:11]
-    dw_buf, rk_buf, b1, b2, ssem, rsem, own, ksend, krecv = refs[11:]
+    dw_buf, rk_buf, piece, b1, b2, ssem, rsem, own, ksend, krecv, tsend, trecv = refs[11:]
     rows = q_ref.shape[0]
     kvh = heads // groups
-    offsets = grid_offsets(nf, nz)
-    greet([grid_peer(nf, nz, a, b) for a, b in offsets])
-    me = lax.axis_index("fsdp") * nz + lax.axis_index("ctx")
-    copies = []
-    for i, (src, buf) in enumerate(((g1_ref, b1), (g2_ref, b2))):
-        for a, b in offsets:
-            target = ring("fsdp", nf, a) * nz + ring("ctx", nz, b)
-            slot = a * nz + b
-            copies.append(
-                remote(src.at[target], buf.at[slot], ssem.at[i, slot], rsem.at[i, slot],
-                       grid_peer(nf, nz, a, b))
-            )
-    mine = [local(g1_ref.at[me], b1.at[0], own.at[0]), local(g2_ref.at[me], b2.at[0], own.at[1])]
+    greet([{"ctx": ring("ctx", nz, o)} for o in range(1, nz)] + across(nt))
+    me = lax.axis_index("ctx")
+    copies = [
+        remote(src.at[ring("ctx", nz, o)], buf.at[o], ssem.at[i, o], rsem.at[i, o],
+               {"ctx": ring("ctx", nz, o)})
+        for i, (src, buf) in enumerate(((g1_ref, b1), (g2_ref, b2)))
+        for o in range(1, nz)
+    ]
     window = (back + 1) * rows
     kvw = kvw_ref[...].reshape(window, kvw_ref.shape[2])
     dks, dvs, dqs = [], [], []
@@ -235,46 +291,56 @@
             dqs.append(dot(ds, key, 1, 0))
         dks.append(dk)
         dvs.append(dv)
-    dkv = jnp.concatenate(dks + dvs, axis=1).reshape(back + 1, rows, 2 * kvh * HD)
-    dw_buf[...] = dkv[:back].astype(BF)
+    dkv = jnp.concatenate(dks + dvs, axis=1)
+    quarter = rows // nt
+    t = lax.axis_index("tp")
+    block = pl.ds(pl.multiple_of(t * quarter, quarter), quarter)
+    dw_buf[...] = dkv.reshape(back + 1, rows, 2 * kvh * HD).astype(BF)
     kcopies = [
-        remote(dw_buf.at[back - o], rk_buf.at[o - 1], ksend.at[o], krecv.at[o],
+        remote(dw_buf.at[back - o, block], rk_buf.at[o - 1], ksend.at[o], krecv.at[o],
                {"ctx": ring("ctx", nz, -o)})
         for o in range(1, back + 1)
     ]
     dq_ref[...] = jnp.concatenate(dqs, axis=1) * HD ** (-0.5)
-    finish(mine)
-    finish(kcopies)
-    total = dkv[back]
+    total = dw_buf[back, block].astype(F32)
     for o in range(back):
+        kcopies[o].wait()
         total = total + rk_buf[o].astype(F32)
-    dkv_ref[...] = total
+    piece[...] = total.astype(BF)
+    tcopies = [
+        remote(piece, dkv_ref.at[t], tsend.at[o], trecv.at[o], {"tp": ring("tp", nt, o)})
+        for o in range(1, nt)
+    ]
+    local(piece, dkv_ref.at[t], own).wait()
     finish(copies)
-    for buf, out in ((b1, s1_ref), (b2, s2_ref)):
-        total = buf[0].astype(F32)
-        for i in range(1, nf * nz):
-            total = total + buf[i].astype(F32)
+    for src, buf, out in ((g1_ref, b1, s1_ref), (g2_ref, b2, s2_ref)):
+        total = src[me].astype(F32)
+        for o in range(1, nz):
+            total = total + buf[o].astype(F32)
         out[...] = total.astype(BF)
-
-
-def attend_back(q, kvw, p, att, go, g1, g2, nf, nz, back, heads, groups, cid):
+    finish(tcopies)
+
+
+def attend_back(q, kvw, p, att, go, g1, g2, nz, nt, back, heads, groups, cid):
     rows = q.shape[0]
     sems = pltpu.SemaphoreType.DMA
-    n = nf * nz
+    quarter = rows // nt
     return pl.pallas_call(
-        functools.partial(attend_back_kernel, nf, nz, back, heads, groups),
+        functools.partial(attend_back_kernel, nz, nt, back, heads, groups),
         out_shape=[
             jax.ShapeDtypeStruct(q.shape, F32),
-            jax.ShapeDtypeStruct(kvw.shape[1:], F32),
+            jax.ShapeDtypeStruct((nt, quarter, kvw.shape[2]), BF),
             jax.ShapeDtypeStruct(g1.shape[1:], BF),
             jax.ShapeDtypeStruct(g2.shape[1:], BF),
         ],
         in_specs=[VM] * 7,
         out_specs=[VM] * 4,
         scratch_shapes=[
-            pltpu.VMEM((back,) + kvw.shape[1:], BF), pltpu.VMEM((back,) + kvw.shape[1:], BF),
+            pltpu.VMEM(kvw.shape, BF), pltpu.VMEM((back, quarter, kvw.shape[2]), BF),
+            pltpu.VMEM((quarter, kvw.shape[2]), BF),
             pltpu.VMEM(g1.shape, BF), pltpu.VMEM(g2.shape, BF),
-            sems((2, n)), sems((2, n)), sems((2,)), sems((back + 1,)), sems((back + 1,)),
+            sems((2, nz)), sems((2, nz)), sems(()), sems((back + 1,)), sems((back + 1,)),
+            sems((nt,)), sems((nt,)),
         ],
         compiler_params=pltpu.CompilerParams(collective_id=cid, has_side_effects=True),
         name="attend_back",
@@ -333,13 +399,19 @@
             )
         local(src, dst, own.at[i]).wait()
     finish(late)
+    t = lax.axis_index("tp")
     part = out_ref.at[:, :, columns]
-    finish(
-        [
-            remote(part, part, tsend.at[o], trecv.at[o], {"tp": ring("tp", nt, o)})
-            for o in range(1, nt)
-        ]
-    )
+    hops = [
+        remote(part, part, tsend.at[2 * o], trecv.at[2 * o], {"tp": ring("tp", nt, 2 * o)})
+        for o in range(1, nt // 2)
+    ]
+    swaps = [remote(part, part, tsend.at[0], trecv.at[0], partner())]
+    for o in range(1, nt // 2):
+        hops[o - 1].wait()
+        theirs = lax.rem(t + (nt - 2 * o), nt)
+        got = out_ref.at[:, :, pl.ds(pl.multiple_of(theirs * cols, cols), cols)]
+        swaps.append(remote(got, got, tsend.at[2 * o + 1], trecv.at[2 * o + 1], partner()))
+    finish(swaps)
     finish(gathers)
 
 
@@ -412,26 +484,20 @@
     pos = positions.reshape(rows)
     top = cotangent.reshape(rows, d)
 
-    gains, wq, wkv = first_gather(
-        [jnp.stack([attn_gain, mlp_gain]), query_weight, kv_weight], nf, 1
+    ctab, stab = rotary(pos, heads + kvh, kvh * HD)
+    r1 = inverse_rms(x)
+    head_cols = -(-(dq + dkv) // 256) * 256
+    n1, q, kvw, p, att, gains, wall, wgu, wd = attend(
+        hidden_in.reshape(rows, d), pos[:, None], ctab[:, :dq], stab[:, :dq],
+        jnp.stack([attn_gain, mlp_gain]),
+        jnp.concatenate([query_weight, kv_weight, out_weight], axis=1),
+        gate_up_weight.reshape(-1, 2 * ff), down_weight,
+        nf, nz, nt, back, heads, kvh, head_cols, 2,
     )
     gains = jnp.transpose(gains, (1, 0, 2)).reshape(2, d).astype(F32)
     gain1, gain2 = gains[0], gains[1]
-    wqkv = jnp.concatenate([wq.reshape(d, dq), wkv.reshape(d, dkv)], axis=1)
-    ctab, stab = rotary(pos, heads + kvh, kvh * HD)
-    r1 = inverse_rms(x)
-    n1 = (x * r1 * gain1).astype(BF)
-    raw = dot(n1, wqkv, 1, 0)
-    qkv = (raw * ctab + swap_halves(raw) * stab).astype(BF)
-    q = qkv[:, :dq] * jnp.asarray(HD ** (-0.5), BF)
-    kv = qkv[:, dq:]
-
-    kvw, p, att, wo, wgu, wd = attend(
-        q, kv, pos[:, None],
-        [out_weight, gate_up_weight.reshape(-1, 2 * ff), down_weight],
-        nf, nz, back, heads, groups, 2,
-    )
-    wo = wo.reshape(dq, d)
+    wall = wall.reshape(d, -1)
+    wqkv, wo = wall[:, : dq + dkv], wall[:, dq + dkv :]
     wgu = wgu.reshape(d, 2 * ff)
     wd = wd.reshape(d, ff)
     mid = x + dot(att, wo, 1, 0)
@@ -446,20 +512,23 @@
         [gh * up * sig * (1.0 + gate * (1.0 - sig)), gh * gate * sig], axis=1
     ).astype(BF)
     part = jnp.concatenate([dot(hidden, wd, 1, 1), dot(ggu, wgu, 1, 1)], axis=1).astype(BF)
-    summed = tp_sum(part.reshape(nt, rows // nt, 2 * d), nt, 3).reshape(rows, 2 * d).astype(F32)
+    n = nf * nz
+    down_grad = dot(top, hidden, 0, 0).astype(BF).reshape(nf, nz, d // n, ff)
+    gu_grad = dot(n2, ggu, 0, 0).astype(BF).reshape(nf, nz, d // n, 2 * ff)
+    summed, gu_grad, down_grad = tp_sum(
+        part.reshape(nt, rows // nt, 2 * d), gu_grad, down_grad, nf, nt, 3
+    )
+    summed = summed.reshape(rows, 2 * d).astype(F32)
     block_out = (mid + summed[:, :d]).astype(BF).reshape(1, rows, d)
-    n = nf * nz
-    down_grad = dot(top, hidden, 0, 0).astype(BF).reshape(n, d // n, ff)
-    gu_grad = dot(n2, ggu, 0, 0).astype(BF).reshape(n, d // n, 2 * ff)
     mlp_gain_grad, grad_norm = norm_back(mid, r2, gain2, summed[:, d:])
     grad_mid = top.astype(F32) + grad_norm
     grad_mid_b = grad_mid.astype(BF)
     go = dot(grad_mid_b, wo, 1, 1).astype(BF)
 
     grad_q, grad_kv, s1, s2 = attend_back(
-        q, kvw, p, att, go, gu_grad, down_grad, nf, nz, back, heads, groups, 4
-    )
-    grads = jnp.concatenate([grad_q, grad_kv], axis=1)
+        q, kvw, p, att, go, gu_grad, down_grad, nz, nt, back, heads, groups, 4
+    )
+    grads = jnp.concatenate([grad_q, grad_kv.reshape(rows, dkv).astype(F32)], axis=1)
     grads = (grads * ctab - swap_halves(grads) * stab).astype(BF)
     dw = jnp.concatenate([dot(n1, grads, 0, 0), dot(att, grad_mid_b, 0, 0)], axis=1)
     grad_n1 = dot(grads, wqkv, 1, 1)

time: 217 us -> 173 us (0.80)
  Pallas kernels: 163 us -> 128 us
  other arithmetic: 20.1 us -> 14.3 us
    pallas_call x4 -> x3, Pallas kernels: 118 us -> 84.9 us  [the longest x1 36.9 us: attend(): pl.pallas_call(functools.partial(attend_kernel, nf, nz, nt, back, heads,...]
    dot_general x12 -> x11, matrix products: 12.4 us -> 10.9 us  [dot(): lax.dot_general(a, b, (((ca,), (cb,)), ((), ())), preferred_element_type=...]
    unnamed x59 -> x47, local copies, waits for them, and re-layouts: 5.66 us -> 5.9 us
where the time goes in v2:
time: 173 us; the launch traced here: 172 us
  Pallas kernels  128 us (74%)
  local copies, waits for them, and re-layouts  17.6 us (10%)
  other arithmetic  14.3 us (8%)
  matrix products  10.9 us (6%)
    pallas_call x1, Pallas kernels, last_sum(): pl.pallas_call(functools.partial(last_sum_kernel, nf, nz, nt), out_shape=...  43.5 us
    pallas_call x1, Pallas kernels, attend(): pl.pallas_call(functools.partial(attend_kernel, nf, nz, nt, back, heads,...  36.9 us
    pallas_call x1, Pallas kernels, attend_back(): pl.pallas_call(functools.partial(attend_back_kernel, nz, nt, back, heads,...  27.9 us
    pallas_call x1, Pallas kernels, tp_sum(): pl.pallas_call(functools.partial(tp_sum_kernel, nf, nt), out_shape=[shape...  20.2 us
    dot_general x11, matrix products, dot(): lax.dot_general(a, b, (((ca,), (cb,)), ((), ())), preferred_element_type=...  10.9 us
    unnamed x47, local copies, waits for them, and re-layouts  5.9 us

profile of v2, /device:TPU:0, one launch (start us, length us, event | category | flops | bytes accessed | tf_op | source)
XLA Modules:
  0.0 172.3 jit_solution(12011340294765954659)
XLA Ops:
  0.6 0.7 convert_element_type.87
  1.3 0.2 fusion.30
  1.6 0.1 tile.8
  1.6 0.3 copy.41
  1.9 0.9 slice.86.refs_2_
  2.8 0.1 tile.20
  2.9 0.0 copy-start.12
  2.9 0.0 copy-start.13
  2.9 0.3 copy.42
  3.1 0.0 copy-start
  3.2 0.0 copy-start.9
  3.2 0.9 slice.87.refs_3_
  4.1 1.9 %copy.40 = bf16[1,256,576]{2,1,0:T(8,128)(2,1)} copy(bf16[1,256,576]{1,2,0:T(8,128)(2,1)} %param.11) | data formatting | bytes 589824 | tf_op args[0]
  6.0 2.1 %concatenate.55.refs_5_ = bf16[288,1536]{1,0:T(8,128)(2,1)} concatenate(bf16[288,576]{1,0:T(8,128)(2,1)S(1)} %copy-done.12, bf16[288,384]{1,0:T(8,128)(2,1)} %param.15, bf16[288,576]{1,0:T(8,128)(2,1)S(1)} %copy-done.13), dimensions={1} | concatenate | bytes 1769472 | tf_op jit(solution)/shard_map/concatenate | solution.py:493
  8.1 0.0 copy-done
  8.1 0.8 copy.55
  8.9 0.8 copy.43.refs_1_
  9.7 0.0 copy-done.20
  9.8 0.6 pad_maximum_fusion.5.refs_4_
  10.3 36.9 %attend.1 = (bf16[256,576]{1,0:T(8,128)(2,1)}, bf16[256,576]{1,0:T(8,128)(2,1)}, bf16[3,256,384]{2,1,0:T(8,128)(2,1)}, bf16[9,256,768]{2,1,0:T(8,128)(2,1)}, bf1...) custom-call(bf16[256,576]{1,0:T(8,128)(2,1)} %bitcast.72, ...), custom_call_target="tpu_custom_call" | custom-call | tf_op jit(solution)/shard_map/attend/pallas_call | solution.py:177
  47.3 0.0 copy-start.7
  47.3 2.0 %multiply_reduce_fusion.2 = (f32[256]{0:T(256)S(1)}, f32[256,576]{1,0:T(8,128)S(1)}) fusion(bf16[256,576]{1,0:T(8,128)(2,1)} %get-tuple-element.29.refs_3_, bf16[576,1536]{1,0:T(8,128)(2,1)} %bitcast.86, bf16[1,256,576]{2,1,0:T(8,128)(2,1)S(1)} %copy-done.2), kind=kOutput, calls=%fused_computation.44 | convolution fusion | flops 170458880 | bytes 1950720 | tf_op jit(solution)/shard_map/dot_general | solution.py:20
  49.4 0.1 mul.162
  49.4 0.5 fusion.37
  50.0 0.5 multiply_convert_fusion.2
  50.5 1.4 convolution_convert_fusion.1
  51.9 0.4 convolution_convert_fusion.5
  52.3 0.5 convolution_convert_fusion.4
  52.8 1.0 pad_maximum_fusion.2.x_ref
  53.8 1.1 convolution_convert_fusion.3
  54.9 20.2 %tp_sum.1 = (bf16[4,64,1152]{2,1,0:T(8,128)(2,1)}, bf16[4,72,768]{2,1,0:T(8,128)(2,1)}, bf16[4,72,384]{2,1,0:T(8,128)(2,1)}) custom-call(bf16[4,64,1152]{2,1,0:T(8,128)(2,1)} %pad_maximum_fusion.2.x_ref, bf16[2,4,72,768]{3,2,1,0:T(8,128)(2,1)} %bitcast.74, bf16[2,4,72,384]{3,2,1,0:T(8,128)(2,1)} %bitcast.78), custom_call_target="tpu_custom_call" | custom-call | tf_op jit(solution)/shard_map/tp_sum/pallas_call | solution.py:236
  75.0 1.1 bitcast_convert_fusion.1
  76.2 0.4 multiply_reduce_fusion
  76.6 0.9 copy.45
  77.5 2.0 %subtract_add_fusion = (f32[256,576]{1,0:T(8,128)S(1)}, bf16[1,256,576]{2,1,0:T(8,128)(2,1)}) fusion(f32[256,576]{1,0:T(8,128)S(1)} %get-tuple-element.101, f32[256,1152]{1,0:T(8,128)S(1)} %bitcast_convert_fusion.1, bf16[1,256,576]{2,1,0:T(8,128)(2,1)} %copy.45, f32[256]{0:T(256)S(1)} %broadcast_multiply_fusion.1, f32[256]{0:T(256)S(1)} %get-tuple-element.98, ...), kind=kLoop, calls=%fused_computation.41 | loop fusion | flops 1327104 | bytes 2954496 | tf_op jit(solution)/shard_map/add | solution.py:524
  79.5 1.6 convolution_convert_fusion.6
  81.1 0.9 copy.46.refs_4_
  82.0 27.9 %attend_back.1 = (f32[256,576]{1,0:T(8,128)}, bf16[4,64,384]{2,1,0:T(8,128)(2,1)}, bf16[72,768]{1,0:T(8,128)(2,1)}, bf16[72,384]{1,0:T(8,128)(2,1)}) custom-call(bf16[256,576]{1,0:T(8,128)(2,1)} %get-tuple-element.35.refs_0_, bf16[3,256,384]{2,1,0:T(8,128)(2,1)} %get-tuple-element.36.refs_1_, bf16[9,256,768]{2,1,0:T(8,128)(2,1)} %get-tuple-element.37.refs_2_, ...), custom_call_target="tpu_custom_call" | custom-call | tf_op jit(solution)/shard_map/attend_back/pallas_call | solution.py:328
  109.8 1.0 bitcast_convert_fusion.3
  110.8 1.9 %fusion.3 = (f32[256,928]{1,0:T(8,128)S(1)}, f32[256,928]{1,0:T(8,128)S(1)}) fusion(f32[256,576]{1,0:T(8,128)} %get-tuple-element.40, f32[256,384]{1,0:T(8,128)S(1)} %bitcast_convert_fusion.3), kind=kLoop, calls=%fused_computation.22 | loop fusion | flops 475136 | bytes 2883584 | tf_op jit(solution)/shard_map/concatenate | solution.py:531
  112.7 0.1 slice.96
  112.9 0.0 copy-start.3
  112.9 0.6 fusion.6
  113.5 0.1 mul.184
  113.6 0.3 copy-done.3
  113.8 0.1 fusion.8
  114.0 2.1 %fusion.15 = (f32[576]{0:T(1024)S(1)}, f32[256]{0:T(256)S(1)}, f32[256,576]{1,0:T(8,128)S(1)}) fusion(f32[256]{0:T(256)S(1)} %get-tuple-element.97, bf16[1,256,576]{2,1,0:T(8,128)(2,1)S(1)} %copy-done.3, f32[576]{0:T(1024)S(1)} %mul.184, bf16[256,960]{1,0:T(8,128)(2,1)S(1)} %fusion.6, bf16[576,1536]{1,0:T(8,128)(2,1)} %bitcast.88), kind=kOutput, calls=%fused_computation.37 | convolution fusion | flops 284146880 | bytes 2562560 | tf_op jit(solution)/shard_map/dot_general | solution.py:20
  116.1 0.1 stack.21
  116.2 0.1 stack.22
  116.2 0.6 maximum_bitcast_fusion.refs_1_
  116.9 0.5 convolution_convert_fusion
  117.4 0.4 convolution_convert_fusion.2
  117.8 1.6 pad_maximum_fusion.refs_0_
  119.4 43.5 %last_sum.1 = (bf16[4,72,1536]{2,1,0:T(8,128)(2,1)}, f32[4,2,72]{2,1,0:T(2,128)}, bf16[4,72,768]{2,1,0:T(8,128)(2,1)}, bf16[4,72,384]{2,1,0:T(8,128)(2,1)}) custom-call(bf16[8,72,1536]{2,1,0:T(8,128)(2,1)} %pad_maximum_fusion.refs_0_, f32[8,2,72]{2,1,0:T(2,128)} %maximum_bitcast_fusion.refs_1_, bf16[72,768]{1,0:T(8,128)(2,1)} %get-tuple-element.43.refs_2_, ...), custom_call_target="tpu_custom_call" | custom-call | tf_op jit(solution)/shard_map/last_sum/pallas_call | solution.py:422
  163.0 1.4 bitcast_convert_fusion
  164.4 1.3 fusion.38
  165.7 0.9 slice.103
  166.7 1.4 reshape.163
  168.0 0.8 bitcast_convert_fusion.2
  168.9 0.7 squeeze.6
  169.5 0.7 squeeze.7
  170.2 0.2 fusion.12
  170.4 1.0 copy.52
  171.5 0.9 copy.51
  (47 shorter events, 0.2 us)
Async XLA Ops:
  2.9 3.1 %copy-start.12 = (bf16[288,576]{1,0:T(8,128)(2,1)S(1)}, bf16[288,576]{1,0:T(8,128)(2,1)}, u32[]{:S(2)}) copy-start(bf16[288,576]{1,0:T(8,128)(2,1)} %param.14) | copy-start | bytes 995332
  2.9 3.1 %copy-start.13 = (bf16[288,576]{1,0:T(8,128)(2,1)S(1)}, bf16[288,576]{1,0:T(8,128)(2,1)}, u32[]{:S(2)}) copy-start(bf16[288,576]{1,0:T(8,128)(2,1)} %param.16) | copy-start | bytes 995332
  3.1 5.0 %copy-start = (f32[256,768]{1,0:T(8,128)}, f32[256,768]{1,0:T(8,128)S(1)}, u32[]{:S(2)}) copy-start(f32[256,768]{1,0:T(8,128)S(1)} %copy.42) | copy-start | bytes 2359300
  3.2 5.0 %copy-start.9 = (bf16[288,2,384]{2,1,0:T(2,128)(2,1)S(1)}, bf16[288,2,384]{2,1,0:T(2,128)(2,1)}, u32[]{:S(2)}) copy-start(bf16[288,2,384]{2,1,0:T(2,128)(2,1)} %param.18) | copy-start | bytes 1327108
  4.0 4.9 %copy-start.16 = (s32[1,256]{1,0:T(1,128)S(1)}, s32[1,256]{1,0:T(1,128)}, u32[]{:S(2)}) copy-start(s32[1,256]{1,0:T(1,128)} %param.12) | copy-start | bytes 3076
  4.1 5.7 %copy-start.19 = (bf16[288]{0:T(512)(128)(2,1)S(1)}, bf16[288]{0:T(512)(128)(2,1)}, u32[]{:S(2)}) copy-start(bf16[288]{0:T(512)(128)(2,1)} %param.13) | copy-start | bytes 1732
  4.1 5.7 %copy-start.20 = (bf16[288]{0:T(512)(128)(2,1)S(1)}, bf16[288]{0:T(512)(128)(2,1)}, u32[]{:S(2)}) copy-start(bf16[288]{0:T(512)(128)(2,1)} %param.17) | copy-start | bytes 1732
  8.9 38.3 %copy-start.2 = (bf16[1,256,576]{2,1,0:T(8,128)(2,1)S(1)}, bf16[1,256,576]{2,1,0:T(8,128)(2,1)}, u32[]{:S(2)}) copy-start(bf16[1,256,576]{2,1,0:T(8,128)(2,1)} %copy.40) | copy-start | bytes 884740
  47.2 2.1 %copy-start.18 = (bf16[2,2,288]{2,1,0:T(2,128)(2,1)S(1)}, bf16[2,2,288]{2,1,0:T(2,128)(2,1)}, u32[]{:S(2)}) copy-start(bf16[2,2,288]{2,1,0:T(2,128)(2,1)} %get-tuple-element.31) | copy-start | bytes 6916
  47.2 2.2 %copy-start.8 = (bf16[2,288,768]{2,1,0:T(8,128)(2,1)S(1)}, bf16[2,288,768]{2,1,0:T(8,128)(2,1)}, u32[]{:S(2)}) copy-start(bf16[2,288,768]{2,1,0:T(8,128)(2,1)} %get-tuple-element.32) | copy-start | bytes 2654212
  47.3 2.7 %copy-start.7 = (bf16[1,256,576]{1,2,0:T(8,128)(2,1)S(1)}, bf16[1,256,576]{1,2,0:T(8,128)(2,1)}, u32[]{:S(2)}) copy-start(bf16[1,256,576]{1,2,0:T(8,128)(2,1)} %param.20) | copy-start | bytes 884740
  47.3 2.7 %copy-start.10 = (bf16[2,288,384]{2,1,0:T(8,128)(2,1)S(1)}, bf16[2,288,384]{2,1,0:T(8,128)(2,1)}, u32[]{:S(2)}) copy-start(bf16[2,288,384]{2,1,0:T(8,128)(2,1)} %get-tuple-element.33) | copy-start | bytes 1327108
  110.8 2.0 %copy-start.4 = (f32[256,576]{1,0:T(8,128)S(1)}, f32[256,576]{1,0:T(8,128)}, u32[]{:S(2)}) copy-start(f32[256,576]{1,0:T(8,128)} %get-tuple-element.40) | copy-start | bytes 1769476
  110.8 2.1 %copy-start.1 = (f32[256,768]{1,0:T(8,128)S(1)}, f32[256,768]{1,0:T(8,128)}, u32[]{:S(2)}) copy-start(f32[256,768]{1,0:T(8,128)} %copy-done) | copy-start | bytes 2359300
  112.9 1.0 copy-start.3
  114.0 2.9 %copy-start.14 = (bf16[256,576]{1,0:T(8,128)(2,1)S(1)}, bf16[256,576]{1,0:T(8,128)(2,1)}, u32[]{:S(2)}) copy-start(bf16[256,576]{1,0:T(8,128)(2,1)} %get-tuple-element.42) | copy-start | bytes 884740
  116.1 1.3 copy-start.5
  164.4 2.3 %copy-start.11 = (bf16[4,72,768]{2,1,0:T(8,128)(2,1)S(1)}, bf16[4,72,768]{2,1,0:T(8,128)(2,1)}, u32[]{:S(2)}) copy-start(bf16[4,72,768]{2,1,0:T(8,128)(2,1)} %get-tuple-element.47) | copy-start | bytes 1327108
  165.7 2.3 %copy-start.15 = (bf16[4,72,384]{2,1,0:T(8,128)(2,1)S(1)}, bf16[4,72,384]{2,1,0:T(8,128)(2,1)}, u32[]{:S(2)}) copy-start(bf16[4,72,384]{2,1,0:T(8,128)(2,1)} %get-tuple-element.48) | copy-start | bytes 663556
  165.7 3.2 %copy-start.17 = (f32[4,2,72]{2,1,0:T(2,128)S(1)}, f32[4,2,72]{2,1,0:T(2,128)}, u32[]{:S(2)}) copy-start(f32[4,2,72]{2,1,0:T(2,128)} %get-tuple-element.45) | copy-start | bytes 6916
  170.2 1.3 copy-start.6

commit v3 on v2

--- a/solution.py
+++ b/solution.py
@@ -349,57 +349,104 @@
 
 def last_sum_kernel(nf, nz, nt, *refs):
     w_ref, v_ref, s1_ref, s2_ref, out_ref, vout_ref, o1_ref, o2_ref = refs[:8]
-    buf, vbuf, piece, vpiece, ssem, rsem, own, gsend, grecv, tsend, trecv = refs[8:]
+    wy, wmid, wz, vbuf, piece, vpiece = refs[8:14]
+    ysend, yrecv, zsend, zrecv, vsend, vrecv, own, gsend, grecv, rsend, rrecv, tsend, trecv = refs[14:]
     offsets = grid_offsets(nf, nz)
     z = lax.axis_index("ctx")
+    f = lax.axis_index("fsdp")
+    t = lax.axis_index("tp")
     cols = piece.shape[1]
-    columns = pl.ds(pl.multiple_of(lax.axis_index("tp") * cols, cols), cols)
-    greet(
-        [grid_peer(nf, nz, a, b) for a, b in offsets]
-        + [{"tp": ring("tp", nt, o)} for o in range(1, nt)]
-    )
-    me = lax.axis_index("fsdp") * nz + z
-    copies = []
+    columns = pl.ds(pl.multiple_of(t * cols, cols), cols)
+    greet([grid_peer(nf, nz, a, b) for a, b in offsets] + across(nt))
+    steps = [
+        remote(w_ref.at[ring("fsdp", nf, o), :, :, columns], wy.at[o], ysend.at[o], yrecv.at[o],
+               {"fsdp": ring("fsdp", nf, o)})
+        for o in range(1, nf)
+    ]
+    mine = [
+        local(w_ref.at[f, :, :, columns], wy.at[0], own.at[0]),
+        local(s1_ref, o1_ref.at[z], own.at[1]),
+        local(s2_ref, o2_ref.at[z], own.at[2]),
+    ]
+    vcopies = []
     for a, b in offsets:
         target = ring("fsdp", nf, a) * nz + ring("ctx", nz, b)
         slot = a * nz + b
-        peer = grid_peer(nf, nz, a, b)
-        copies.append(
-            remote(w_ref.at[target, :, columns], buf.at[slot], ssem.at[0, slot], rsem.at[0, slot], peer)
+        vcopies.append(
+            remote(v_ref.at[target], vbuf.at[slot], vsend.at[slot], vrecv.at[slot],
+                   grid_peer(nf, nz, a, b))
         )
-        copies.append(
-            remote(v_ref.at[target], vbuf.at[slot], ssem.at[1, slot], rsem.at[1, slot], peer)
+    both = [(d, i, ref) for d in (0, 1) for i, ref in enumerate((o1_ref, o2_ref))]
+
+    def inside(index):
+        return (index >= 0) & (index < nz)
+
+    def handle(d, i, ref, k, index, device):
+        part = ref.at[index]
+        return pltpu.make_async_remote_copy(
+            src_ref=part, dst_ref=part, send_sem=rsend.at[d, i, k], recv_sem=rrecv.at[d, i, k],
+            device_id={"ctx": device}, device_id_type=MESH,
         )
-    mine = [
-        local(w_ref.at[me, :, columns], buf.at[0], own.at[0]),
-        local(v_ref.at[me], vbuf.at[0], own.at[1]),
-        local(s1_ref, o1_ref.at[z], own.at[2]),
-        local(s2_ref, o2_ref.at[z], own.at[3]),
-    ]
-    gathers = []
-    for i, (src, dst) in enumerate(((s1_ref, o1_ref), (s2_ref, o2_ref))):
-        for o in range(1, nz):
-            gathers.append(
-                remote(src, dst.at[z], gsend.at[i, o], grecv.at[i, o], {"ctx": ring("ctx", nz, o)})
-            )
+
+    def relay(k, act):
+        for d, i, ref in both:
+            way = 1 - 2 * d
+
+            @pl.when(inside(z + way) & inside(z - way * k))
+            def _(d=d, i=i, ref=ref, way=way):
+                copy = handle(d, i, ref, k, z - way * k, z + way)
+                if act == "start":
+                    copy.start()
+                else:
+                    copy.wait_send()
+
+    def arrive(k):
+        for d, i, ref in both:
+            way = 1 - 2 * d
+
+            @pl.when(inside(z - way * (k + 1)))
+            def _(d=d, i=i, ref=ref, way=way):
+                handle(d, i, ref, k, z - way * (k + 1), ring("ctx", nz, 1)).wait_recv()
+
     finish(mine)
-    finish(copies)
-    for source, target in ((buf, piece), (vbuf, vpiece)):
-        total = source[0].astype(F32)
-        for i in range(1, nf * nz):
-            total = total + source[i].astype(F32)
-        target[...] = total.astype(target.dtype)
+    relay(0, "start")
+    finish(steps)
+    total = wy[0].astype(F32)
+    for o in range(1, nf):
+        total = total + wy[o].astype(F32)
+    wmid[...] = total.astype(BF)
+    steps = [
+        remote(wmid.at[ring("ctx", nz, o)], wz.at[o], zsend.at[o], zrecv.at[o],
+               {"ctx": ring("ctx", nz, o)})
+        for o in range(1, nz)
+    ]
+    arrive(0)
+    if nz > 2:
+        relay(1, "start")
+    finish(vcopies)
+    total = v_ref[f * nz + z]
+    for i in range(1, nf * nz):
+        total = total + vbuf[i]
+    vpiece[...] = total
+    finish(steps)
+    total = wmid[z].astype(F32)
+    for o in range(1, nz):
+        total = total + wz[o].astype(F32)
+    piece[...] = total.astype(BF)
     late = []
     for i, (src, dst) in enumerate(
         ((piece, out_ref.at[z, :, columns]), (vpiece, vout_ref.at[z]))
     ):
         for o in range(1, nz):
             late.append(
-                remote(src, dst, gsend.at[2 + i, o], grecv.at[2 + i, o], {"ctx": ring("ctx", nz, o)})
+                remote(src, dst, gsend.at[i, o], grecv.at[i, o], {"ctx": ring("ctx", nz, o)})
             )
         local(src, dst, own.at[i]).wait()
+    for k in range(1, nz - 1):
+        arrive(k)
+        if k + 1 < nz - 1:
+            relay(k + 1, "start")
     finish(late)
-    t = lax.axis_index("tp")
     part = out_ref.at[:, :, columns]
     hops = [
         remote(part, part, tsend.at[2 * o], trecv.at[2 * o], {"tp": ring("tp", nt, 2 * o)})
@@ -412,13 +459,15 @@
         got = out_ref.at[:, :, pl.ds(pl.multiple_of(theirs * cols, cols), cols)]
         swaps.append(remote(got, got, tsend.at[2 * o + 1], trecv.at[2 * o + 1], partner()))
     finish(swaps)
-    finish(gathers)
+    for k in range(nz - 1):
+        relay(k, "end")
 
 
 def last_sum(w, v, s1, s2, nf, nz, nt, cid):
     sems = pltpu.SemaphoreType.DMA
-    n, rows, cols = w.shape
+    rows, cols = w.shape[2:]
     part = cols // nt
+    n = nf * nz
     return pl.pallas_call(
         functools.partial(last_sum_kernel, nf, nz, nt),
         out_shape=[
@@ -430,10 +479,12 @@
         in_specs=[VM] * 4,
         out_specs=[VM] * 4,
         scratch_shapes=[
-            pltpu.VMEM((n, rows, part), BF), pltpu.VMEM(v.shape, F32),
+            pltpu.VMEM((nf, nz, rows, part), BF), pltpu.VMEM((nz, rows, part), BF),
+            pltpu.VMEM((nz, rows, part), BF), pltpu.VMEM(v.shape, F32),
             pltpu.VMEM((rows, part), BF), pltpu.VMEM(v.shape[1:], F32),
-            sems((2, n)), sems((2, n)), sems((4,)),
-            sems((4, nz)), sems((4, nz)), sems((nt,)), sems((nt,)),
+            sems((nf,)), sems((nf,)), sems((nz,)), sems((nz,)), sems((n,)), sems((n,)),
+            sems((3,)), sems((2, nz)), sems((2, nz)), sems((2, 2, nz)), sems((2, 2, nz)),
+            sems((nt,)), sems((nt,)),
         ],
         compiler_params=pltpu.CompilerParams(collective_id=cid, has_side_effects=True),
         name="last_sum",
@@ -538,7 +589,7 @@
         jnp.stack([attn_gain_grad, mlp_gain_grad]).reshape(2, n, d // n), (1, 0, 2)
     )
     out, gout, o1, o2 = last_sum(
-        dw.astype(BF).reshape(n, d // n, -1), gain_grads, s1, s2, nf, nz, nt, 5
+        dw.astype(BF).reshape(nf, nz, d // n, -1), gain_grads, s1, s2, nf, nz, nt, 5
     )
     local_d = d // nf
     out = out.reshape(local_d, -1).astype(F32)

time: 173 us -> 164 us (0.948)
  Pallas kernels: 128 us -> 120 us
    pallas_call x1, Pallas kernels: 43.5 us -> 34.7 us  [last_sum(): pl.pallas_call(functools.partial(last_sum_kernel, nf, nz, nt), out_shape=...]
where the time goes in v3:
time: 164 us
  Pallas kernels  120 us (73%)
  local copies, waits for them, and re-layouts  17.6 us (11%)
  other arithmetic  14.3 us (9%)
  matrix products  10.9 us (7%)
    pallas_call x1, Pallas kernels, attend(): pl.pallas_call(functools.partial(attend_kernel, nf, nz, nt, back, heads,...  36.9 us
    pallas_call x1, Pallas kernels, last_sum(): pl.pallas_call(functools.partial(last_sum_kernel, nf, nz, nt), out_shape=...  34.7 us
    pallas_call x1, Pallas kernels, attend_back(): pl.pallas_call(functools.partial(attend_back_kernel, nz, nt, back, heads,...  27.9 us
    pallas_call x1, Pallas kernels, tp_sum(): pl.pallas_call(functools.partial(tp_sum_kernel, nf, nt), out_shape=[shape...  20.2 us
    dot_general x11, matrix products, dot(): lax.dot_general(a, b, (((ca,), (cb,)), ((), ())), preferred_element_type=...  10.9 us
    unnamed x47, local copies, waits for them, and re-layouts  5.9 us

profile of v3, /device:TPU:0, one launch (start us, length us, event | category | flops | bytes accessed | tf_op | source)
XLA Modules:
  0.0 163.5 jit_solution(7568066009148840694)
XLA Ops:
  0.6 0.7 convert_element_type.87
  1.3 0.2 fusion.30
  1.6 0.1 tile.8
  1.6 0.3 copy.41
  1.9 0.9 slice.86.refs_2_
  2.8 0.1 tile.20
  2.9 0.0 copy-start.12
  2.9 0.0 copy-start.13
  2.9 0.3 copy.42
  3.2 0.0 copy-start.9
  3.2 0.9 slice.87.refs_3_
  4.1 1.9 %copy.40 = bf16[1,256,576]{2,1,0:T(8,128)(2,1)} copy(bf16[1,256,576]{1,2,0:T(8,128)(2,1)} %param.11) | data formatting | bytes 589824 | tf_op args[0]
  6.0 0.0 copy-done.13
  6.0 2.1 %concatenate.55.refs_5_ = bf16[288,1536]{1,0:T(8,128)(2,1)} concatenate(bf16[288,576]{1,0:T(8,128)(2,1)S(1)} %copy-done.12, bf16[288,384]{1,0:T(8,128)(2,1)} %param.15, bf16[288,576]{1,0:T(8,128)(2,1)S(1)} %copy-done.13), dimensions={1} | concatenate | bytes 1769472 | tf_op jit(solution)/shard_map/concatenate | solution.py:544
  8.1 0.8 copy.55
  8.9 0.8 copy.43.refs_1_
  9.8 0.6 pad_maximum_fusion.5.refs_4_
  10.3 36.9 %attend.1 = (bf16[256,576]{1,0:T(8,128)(2,1)}, bf16[256,576]{1,0:T(8,128)(2,1)}, bf16[3,256,384]{2,1,0:T(8,128)(2,1)}, bf16[9,256,768]{2,1,0:T(8,128)(2,1)}, bf1...) custom-call(bf16[256,576]{1,0:T(8,128)(2,1)} %bitcast.72, ...), custom_call_target="tpu_custom_call" | custom-call | tf_op jit(solution)/shard_map/attend/pallas_call | solution.py:177
  47.3 0.0 copy-start.7
  47.3 2.0 %multiply_reduce_fusion.2 = (f32[256]{0:T(256)S(1)}, f32[256,576]{1,0:T(8,128)S(1)}) fusion(bf16[256,576]{1,0:T(8,128)(2,1)} %get-tuple-element.29.refs_3_, bf16[576,1536]{1,0:T(8,128)(2,1)} %bitcast.86, bf16[1,256,576]{2,1,0:T(8,128)(2,1)S(1)} %copy-done.2), kind=kOutput, calls=%fused_computation.44 | convolution fusion | flops 170458880 | bytes 1950720 | tf_op jit(solution)/shard_map/dot_general | solution.py:20
  49.4 0.1 mul.162
  49.4 0.0 copy-done.8
  49.4 0.5 fusion.37
  50.0 0.0 copy-done.7
  50.0 0.5 multiply_convert_fusion.2
  50.5 1.4 convolution_convert_fusion.1
  51.9 0.4 convolution_convert_fusion.5
  52.3 0.5 convolution_convert_fusion.4
  52.8 1.0 pad_maximum_fusion.2.x_ref
  53.8 1.1 convolution_convert_fusion.3
  54.9 20.2 %tp_sum.1 = (bf16[4,64,1152]{2,1,0:T(8,128)(2,1)}, bf16[4,72,768]{2,1,0:T(8,128)(2,1)}, bf16[4,72,384]{2,1,0:T(8,128)(2,1)}) custom-call(bf16[4,64,1152]{2,1,0:T(8,128)(2,1)} %pad_maximum_fusion.2.x_ref, bf16[2,4,72,768]{3,2,1,0:T(8,128)(2,1)} %bitcast.74, bf16[2,4,72,384]{3,2,1,0:T(8,128)(2,1)} %bitcast.78), custom_call_target="tpu_custom_call" | custom-call | tf_op jit(solution)/shard_map/tp_sum/pallas_call | solution.py:236
  75.0 1.1 bitcast_convert_fusion.1
  76.2 0.4 multiply_reduce_fusion
  76.6 0.9 copy.45
  77.5 2.0 %subtract_add_fusion = (f32[256,576]{1,0:T(8,128)S(1)}, bf16[1,256,576]{2,1,0:T(8,128)(2,1)}) fusion(f32[256,576]{1,0:T(8,128)S(1)} %get-tuple-element.101, f32[256,1152]{1,0:T(8,128)S(1)} %bitcast_convert_fusion.1, bf16[1,256,576]{2,1,0:T(8,128)(2,1)} %copy.45, f32[256]{0:T(256)S(1)} %broadcast_multiply_fusion.1, f32[256]{0:T(256)S(1)} %get-tuple-element.98, ...), kind=kLoop, calls=%fused_computation.41 | loop fusion | flops 1327104 | bytes 2954496 | tf_op jit(solution)/shard_map/add | solution.py:575
  79.5 1.6 convolution_convert_fusion.6
  81.1 0.9 copy.46.refs_4_
  82.0 27.9 %attend_back.1 = (f32[256,576]{1,0:T(8,128)}, bf16[4,64,384]{2,1,0:T(8,128)(2,1)}, bf16[72,768]{1,0:T(8,128)(2,1)}, bf16[72,384]{1,0:T(8,128)(2,1)}) custom-call(bf16[256,576]{1,0:T(8,128)(2,1)} %get-tuple-element.35.refs_0_, bf16[3,256,384]{2,1,0:T(8,128)(2,1)} %get-tuple-element.36.refs_1_, bf16[9,256,768]{2,1,0:T(8,128)(2,1)} %get-tuple-element.37.refs_2_, ...), custom_call_target="tpu_custom_call" | custom-call | tf_op jit(solution)/shard_map/attend_back/pallas_call | solution.py:328
  109.8 1.0 bitcast_convert_fusion.3
  110.8 1.9 %fusion.3 = (f32[256,928]{1,0:T(8,128)S(1)}, f32[256,928]{1,0:T(8,128)S(1)}) fusion(f32[256,576]{1,0:T(8,128)} %get-tuple-element.40, f32[256,384]{1,0:T(8,128)S(1)} %bitcast_convert_fusion.3), kind=kLoop, calls=%fused_computation.22 | loop fusion | flops 475136 | bytes 2883584 | tf_op jit(solution)/shard_map/concatenate | solution.py:582
  112.7 0.1 slice.96
  112.9 0.0 copy-start.3
  112.9 0.6 fusion.6
  113.5 0.1 mul.184
  113.6 0.3 copy-done.3
  113.8 0.1 fusion.8
  114.0 2.1 %fusion.15 = (f32[576]{0:T(1024)S(1)}, f32[256]{0:T(256)S(1)}, f32[256,576]{1,0:T(8,128)S(1)}) fusion(f32[256]{0:T(256)S(1)} %get-tuple-element.97, bf16[1,256,576]{2,1,0:T(8,128)(2,1)S(1)} %copy-done.3, f32[576]{0:T(1024)S(1)} %mul.184, bf16[256,960]{1,0:T(8,128)(2,1)S(1)} %fusion.6, bf16[576,1536]{1,0:T(8,128)(2,1)} %bitcast.88), kind=kOutput, calls=%fused_computation.37 | convolution fusion | flops 284146880 | bytes 2562560 | tf_op jit(solution)/shard_map/dot_general | solution.py:20
  116.1 0.1 stack.21
  116.2 0.1 stack.22
  116.2 0.6 maximum_bitcast_fusion.refs_1_
  116.9 0.5 convolution_convert_fusion
  117.4 0.4 convolution_convert_fusion.2
  117.8 1.6 %pad_maximum_fusion.refs_0_ = bf16[2,4,72,1536]{3,2,1,0:T(8,128)(2,1)} fusion(bf16[2,4,72,576]{3,2,1,0:T(8,128)(2,1)S(1)} %bitcast.77, bf16[2,4,72,960]{3,2,1,0:T(8,128)(2,1)S(1)} %bitcast.73), kind=kLoop, calls=%fused_computation | loop fusion | flops 3538944 | bytes 3538944 | tf_op jit(solution)/shard_map/concatenate | solution.py:584
  119.4 34.7 %last_sum.1 = (bf16[4,72,1536]{2,1,0:T(8,128)(2,1)}, f32[4,2,72]{2,1,0:T(2,128)}, bf16[4,72,768]{2,1,0:T(8,128)(2,1)}, bf16[4,72,384]{2,1,0:T(8,128)(2,1)}) custom-call(bf16[2,4,72,1536]{3,2,1,0:T(8,128)(2,1)} %pad_maximum_fusion.refs_0_, f32[8,2,72]{2,1,0:T(2,128)} %maximum_bitcast_fusion.refs_1_, bf16[72,768]{1,0:T(8,128)(2,1)} %get-tuple-element.43.refs_2_, ...), custom_call_target="tpu_custom_call" | custom-call | tf_op jit(solution)/shard_map/last_sum/pallas_call | solution.py:471
  154.2 1.4 bitcast_convert_fusion
  155.6 1.3 fusion.38
  156.9 0.9 slice.103
  157.9 1.4 reshape.163
  159.2 0.8 bitcast_convert_fusion.2
  160.1 0.7 squeeze.6
  160.8 0.7 squeeze.7
  161.4 0.2 fusion.12
  161.6 1.0 copy.52
  162.7 0.9 copy.51
  (47 shorter events, 0.2 us)
Async XLA Ops:
  2.9 3.1 %copy-start.12 = (bf16[288,576]{1,0:T(8,128)(2,1)S(1)}, bf16[288,576]{1,0:T(8,128)(2,1)}, u32[]{:S(2)}) copy-start(bf16[288,576]{1,0:T(8,128)(2,1)} %param.14) | copy-start | bytes 995332
  2.9 3.1 %copy-start.13 = (bf16[288,576]{1,0:T(8,128)(2,1)S(1)}, bf16[288,576]{1,0:T(8,128)(2,1)}, u32[]{:S(2)}) copy-start(bf16[288,576]{1,0:T(8,128)(2,1)} %param.16) | copy-start | bytes 995332
  3.1 5.0 %copy-start = (f32[256,768]{1,0:T(8,128)}, f32[256,768]{1,0:T(8,128)S(1)}, u32[]{:S(2)}) copy-start(f32[256,768]{1,0:T(8,128)S(1)} %copy.42) | copy-start | bytes 2359300
  3.2 5.0 %copy-start.9 = (bf16[288,2,384]{2,1,0:T(2,128)(2,1)S(1)}, bf16[288,2,384]{2,1,0:T(2,128)(2,1)}, u32[]{:S(2)}) copy-start(bf16[288,2,384]{2,1,0:T(2,128)(2,1)} %param.18) | copy-start | bytes 1327108
  4.0 4.9 %copy-start.16 = (s32[1,256]{1,0:T(1,128)S(1)}, s32[1,256]{1,0:T(1,128)}, u32[]{:S(2)}) copy-start(s32[1,256]{1,0:T(1,128)} %param.12) | copy-start | bytes 3076
  4.1 5.7 %copy-start.19 = (bf16[288]{0:T(512)(128)(2,1)S(1)}, bf16[288]{0:T(512)(128)(2,1)}, u32[]{:S(2)}) copy-start(bf16[288]{0:T(512)(128)(2,1)} %param.13) | copy-start | bytes 1732
  4.1 5.7 %copy-start.20 = (bf16[288]{0:T(512)(128)(2,1)S(1)}, bf16[288]{0:T(512)(128)(2,1)}, u32[]{:S(2)}) copy-start(bf16[288]{0:T(512)(128)(2,1)} %param.17) | copy-start | bytes 1732
  8.9 38.3 %copy-start.2 = (bf16[1,256,576]{2,1,0:T(8,128)(2,1)S(1)}, bf16[1,256,576]{2,1,0:T(8,128)(2,1)}, u32[]{:S(2)}) copy-start(bf16[1,256,576]{2,1,0:T(8,128)(2,1)} %copy.40) | copy-start | bytes 884740
  47.2 2.1 %copy-start.18 = (bf16[2,2,288]{2,1,0:T(2,128)(2,1)S(1)}, bf16[2,2,288]{2,1,0:T(2,128)(2,1)}, u32[]{:S(2)}) copy-start(bf16[2,2,288]{2,1,0:T(2,128)(2,1)} %get-tuple-element.31) | copy-start | bytes 6916
  47.2 2.2 %copy-start.8 = (bf16[2,288,768]{2,1,0:T(8,128)(2,1)S(1)}, bf16[2,288,768]{2,1,0:T(8,128)(2,1)}, u32[]{:S(2)}) copy-start(bf16[2,288,768]{2,1,0:T(8,128)(2,1)} %get-tuple-element.32) | copy-start | bytes 2654212
  47.3 2.7 %copy-start.7 = (bf16[1,256,576]{1,2,0:T(8,128)(2,1)S(1)}, bf16[1,256,576]{1,2,0:T(8,128)(2,1)}, u32[]{:S(2)}) copy-start(bf16[1,256,576]{1,2,0:T(8,128)(2,1)} %param.20) | copy-start | bytes 884740
  47.3 2.7 %copy-start.10 = (bf16[2,288,384]{2,1,0:T(8,128)(2,1)S(1)}, bf16[2,288,384]{2,1,0:T(8,128)(2,1)}, u32[]{:S(2)}) copy-start(bf16[2,288,384]{2,1,0:T(8,128)(2,1)} %get-tuple-element.33) | copy-start | bytes 1327108
  110.8 2.0 %copy-start.4 = (f32[256,576]{1,0:T(8,128)S(1)}, f32[256,576]{1,0:T(8,128)}, u32[]{:S(2)}) copy-start(f32[256,576]{1,0:T(8,128)} %get-tuple-element.40) | copy-start | bytes 1769476
  110.8 2.1 %copy-start.1 = (f32[256,768]{1,0:T(8,128)S(1)}, f32[256,768]{1,0:T(8,128)}, u32[]{:S(2)}) copy-start(f32[256,768]{1,0:T(8,128)} %copy-done) | copy-start | bytes 2359300
  112.9 1.0 copy-start.3
  114.0 2.9 %copy-start.14 = (bf16[256,576]{1,0:T(8,128)(2,1)S(1)}, bf16[256,576]{1,0:T(8,128)(2,1)}, u32[]{:S(2)}) copy-start(bf16[256,576]{1,0:T(8,128)(2,1)} %get-tuple-element.42) | copy-start | bytes 884740
  116.1 1.3 copy-start.5
  155.6 2.3 %copy-start.11 = (bf16[4,72,768]{2,1,0:T(8,128)(2,1)S(1)}, bf16[4,72,768]{2,1,0:T(8,128)(2,1)}, u32[]{:S(2)}) copy-start(bf16[4,72,768]{2,1,0:T(8,128)(2,1)} %get-tuple-element.47) | copy-start | bytes 1327108
  156.9 2.3 %copy-start.15 = (bf16[4,72,384]{2,1,0:T(8,128)(2,1)S(1)}, bf16[4,72,384]{2,1,0:T(8,128)(2,1)}, u32[]{:S(2)}) copy-start(bf16[4,72,384]{2,1,0:T(8,128)(2,1)} %get-tuple-element.48) | copy-start | bytes 663556
  156.9 3.2 %copy-start.17 = (f32[4,2,72]{2,1,0:T(2,128)S(1)}, f32[4,2,72]{2,1,0:T(2,128)}, u32[]{:S(2)}) copy-start(f32[4,2,72]{2,1,0:T(2,128)} %get-tuple-element.45) | copy-start | bytes 6916
  161.4 1.3 copy-start.6
